TPU v7x, 32 devices: a whole 2x2x4 slice. The times are simulated.
32 devices in a mesh: space: 4 (over x, core), chan: 8 (over z, y).
Axes of the slice: x: 2, y: 2, z: 4, core: 2. Of those that a mesh axis runs over, the one named last changes fastest.
Arguments:
- grid_in: bfloat16 [227, 32768], P(None, ('space', 'chan')), may hold values from -6 to 6
- grid_embed_w: bfloat16 [512, 227], replicated, may hold values from -0.375 to 0.375
- g2m_w: bfloat16 [512, 512], replicated, may hold values from -0.25 to 0.25
- pair_w: bfloat16 [4, 2, 512, 512], replicated, may hold values from -0.25 to 0.25
- second_w: bfloat16 [5, 512, 512], replicated, may hold values from -0.25 to 0.25
- first_b: float32 [6, 512], replicated, may hold values from -4 to 4
- norm_gain: float32 [5, 512], replicated, may hold values from 0.5 to 1.5
- geom_w: bfloat16 [3, 512, 4], replicated, may hold values from -3 to 3
- out_w: bfloat16 [227, 512], replicated, may hold values from -0.25 to 0.25
- out_b: float32 [227], replicated, may hold values from -4 to 4
- g2m_geom: bfloat16 [4, 49152], P(None, ('space', 'chan')), may hold values from -6 to 6
- mesh_geom: bfloat16 [4, 65536], P(None, ('space', 'chan')), may hold values from -6 to 6
- m2g_geom: bfloat16 [4, 98304], P(None, ('space', 'chan')), may hold values from -6 to 6
- g2m_send: int32 [49152], P(('space', 'chan')), may hold values from 0 to 32767, as said below
- g2m_recv: int32 [49152], P(('space', 'chan')), may hold values from 0 to 16383, as said below
- mesh_recv: int32 [65536], P(('space', 'chan')), may hold values from 0 to 16383, as said below
- mesh_slot: int32 [65536], P(('space', 'chan')), may hold values from 0 to 2047
- mesh_rows: int32 [1024, 64], P(('space', 'chan')), may hold values from 0 to 511
- m2g_send: int32 [98304], P(('space', 'chan')), may hold values from 0 to 16383, as said below
Outputs:
- prediction: float32 [227, 32768], P(None, ('space', 'chan'))
- mesh_state: bfloat16 [512, 16384], P(None, ('space', 'chan'))
Inputs may be any that keep to these rules, and one draw needn't show every extreme that they name: `g2m_send`: the edges of block d (1536 edges each) send from grid cells d * 1024 - 256 to (d + 1) * 1024 + 255, within the grid. `g2m_recv`: the edges of block d (1536 edges each) end at mesh nodes d * 512 to (d + 1) * 512 - 1. `mesh_recv`: the edges of block d (2048 edges each) end at mesh nodes d * 512 to (d + 1) * 512 - 1. `m2g_send`: for grid cell g in block d = g // 1024, the edges 3g to 3g + 2 send from mesh nodes d * 512 - 128 to (d + 1) * 512 + 127, within the mesh.
All inputs are finite; a program needn't handle non-finite values.
Results may differ from a plain program's by a relative error of at most 0.0095.
Values may be sent and summed in bfloat16 or wider, within the bound.
No kernel may reach another device: no remote copies, remote signals or barrier semaphores. Data moves between devices by JAX's collectives and lax.ppermute only.
A program may use at most 128 MiB of HBM per device.

v0:
```python
import jax
import jax.numpy as jnp
from jax import lax
from jax.sharding import PartitionSpec as P

M_DEV = 512


eps = 1e-05


def padded(block, sides, width):
    for axis, dim in sides:
        count = lax.axis_size(axis)
        forward = [(i, i + 1) for i in range(count - 1)]
        backward = [(target, source) for source, target in forward]
        low = lax.ppermute(
            lax.slice_in_dim(block, block.shape[dim] - width, None, axis=dim), axis, forward
        )
        high = lax.ppermute(lax.slice_in_dim(block, 0, width, axis=dim), axis, backward)
        block = jnp.concatenate([low, block, high], axis=dim)
    return block


def by_rows(values, weight):
    return lax.dot_general(
        values, weight, (((1,), (1,)), ((), ())), preferred_element_type=jnp.float32
    )


def by_columns(values, weight):
    return lax.dot_general(
        values, weight, (((0,), (1,)), ((), ())), preferred_element_type=jnp.float32
    )


def layer_norm(values, gain_rows):
    row_mean = jnp.mean(values, axis=1)
    row_var = jnp.mean(values * values, axis=1) - row_mean * row_mean
    return (values - row_mean[:, None]) * lax.rsqrt(row_var + eps)[:, None] * gain_rows[None, :]


def edge_block(pre_act, weight, gain_rows):
    hidden = jax.nn.silu(pre_act).astype(jnp.bfloat16)
    return layer_norm(by_rows(hidden, weight), gain_rows).astype(jnp.bfloat16)


def sum_to_nodes(message, receivers, node_count):
    one_hot = (receivers[:, None] == jnp.arange(node_count, dtype=jnp.int32)[None, :]).astype(
        jnp.bfloat16
    )
    return lax.dot_general(
        one_hot, message, (((0,), (0,)), ((), ())), preferred_element_type=jnp.float32
    )


def body(
    grid_in,
    grid_embed_w,
    g2m_w,
    pair_w,
    second_w,
    first_b,
    norm_gain,
    geom_w,
    out_w,
    out_b,
    g2m_geom,
    mesh_geom,
    m2g_geom,
    g2m_send,
    g2m_recv,
    mesh_recv,
    mesh_slot,
    mesh_rows,
    m2g_send,
):
    width = grid_embed_w.shape[0]
    grid_cells = grid_in.shape[1]
    position = lax.axis_index(("space", "chan"))
    grid_latent = edge_block(
        by_columns(grid_in, grid_embed_w) + first_b[0][None, :], second_w[0], norm_gain[0]
    )
    stacked = jnp.concatenate([g2m_w, pair_w[2, 1], pair_w[3, 0]], axis=0)
    grid_terms = by_rows(grid_latent, stacked)
    encode_send = grid_terms[:, :width].astype(jnp.bfloat16)
    decode_grid = grid_terms[:, width : 2 * width]
    output_grid = grid_terms[:, 2 * width :]
    grid_reach = grid_cells // 4
    extended = padded(encode_send, ((("space", "chan"), 0),), grid_reach)
    sender_local = g2m_send - position * grid_cells + grid_reach
    pre_act = (
        extended[sender_local].astype(jnp.float32)
        + by_columns(g2m_geom, geom_w[0])
        + first_b[1][None, :]
    )
    message = edge_block(pre_act, second_w[1], norm_gain[1])
    mesh_latent = sum_to_nodes(message, g2m_recv - position * M_DEV, M_DEV).astype(jnp.bfloat16)
    link_terms = by_rows(mesh_latent, jnp.concatenate([pair_w[0, 0], pair_w[0, 1]], axis=0))
    link_send = link_terms[:, :width].astype(jnp.bfloat16)
    link_recv = link_terms[:, width:]
    space_count = lax.axis_size("space")
    chan_count = lax.axis_size("chan")
    outgoing = link_send[mesh_rows.reshape(-1)].reshape(space_count * chan_count, -1, width)
    arrived = lax.all_to_all(
        outgoing, ("space", "chan"), split_axis=0, concat_axis=0, tiled=True
    ).reshape(-1, width)
    recv_local = mesh_recv - position * M_DEV
    pre_act = (
        arrived[mesh_slot].astype(jnp.float32)
        + link_recv[recv_local]
        + by_columns(mesh_geom, geom_w[1])
        + first_b[2][None, :]
    )
    message = edge_block(pre_act, second_w[2], norm_gain[2])
    aggregate = sum_to_nodes(message, recv_local, M_DEV).astype(jnp.bfloat16)
    node_pre = (
        by_rows(mesh_latent, pair_w[1, 0]) + by_rows(aggregate, pair_w[1, 1]) + first_b[3][None, :]
    )
    node_hidden = jax.nn.silu(node_pre).astype(jnp.bfloat16)
    state_rows = (
        mesh_latent.astype(jnp.float32)
        + layer_norm(by_rows(node_hidden, second_w[3]), norm_gain[3])
    ).astype(jnp.bfloat16)
    decode_send = by_rows(state_rows, pair_w[2, 0]).astype(jnp.bfloat16)
    mesh_reach = M_DEV // 4
    widened = padded(decode_send, ((("space", "chan"), 0),), mesh_reach)
    mesh_sender = m2g_send - position * M_DEV + mesh_reach
    expanded = jnp.broadcast_to(decode_grid[:, None, :], (grid_cells, 3, width)).reshape(
        3 * grid_cells, width
    )
    pre_act = (
        widened[mesh_sender].astype(jnp.float32)
        + expanded
        + by_columns(m2g_geom, geom_w[2])
        + first_b[4][None, :]
    )
    message = edge_block(pre_act, second_w[4], norm_gain[4])
    gathered = (
        message.astype(jnp.float32).reshape(grid_cells, 3, width).sum(axis=1).astype(jnp.bfloat16)
    )
    out_pre = output_grid + by_rows(gathered, pair_w[3, 1]) + first_b[5][None, :]
    out_hidden = jax.nn.silu(out_pre).astype(jnp.bfloat16)
    prediction = by_rows(out_w, out_hidden) + out_b[:, None]
    return (prediction, state_rows.T)


def solution(mesh):
    return jax.shard_map(
        body,
        mesh=mesh,
        in_specs=(
            P(None, ("space", "chan")),
            P(),
            P(),
            P(),
            P(),
            P(),
            P(),
            P(),
            P(),
            P(),
            P(None, ("space", "chan")),
            P(None, ("space", "chan")),
            P(None, ("space", "chan")),
            P(("space", "chan")),
            P(("space", "chan")),
            P(("space", "chan")),
            P(("space", "chan")),
            P(("space", "chan"), None),
            P(("space", "chan")),
        ),
        out_specs=(P(None, ("space", "chan")), P(None, ("space", "chan"))),
        check_vma=False,
    )
```

profile of v0, /device:TPU:0, one launch (start us, length us, event | category | flops | bytes accessed | tf_op | source)
XLA Modules:
  0.0 193.4 jit_solution(9480164894891578349)
XLA Ops:
  5.4 3.5 %fusion.100 = (f32[1024]{0:T(1024)S(1)}, f32[1024]{0:T(1024)S(1)}, f32[1024,512]{0,1:T(8,128)}) fusion(bf16[5,512,512]{2,1,0:T(8,128)(2,1)} %param.23, bf16[227,1024]{1,0:T(8,128)(2,1)S(1)} %copy-done, bf16[512,227]{0,1:T(8,128)(2,1)S(1)} %copy-done.14, f32[512]{0:T(512)S(1)} %bitcast.109), kind=kOutput, calls=%fused_computation.135 | convolution fusion | flops 779614208 | bytes 3329024 | tf_op jit(solution)/shard_map/dot_general | solution.py:26
  9.0 6.7 %fusion.106 = (bf16[1024,1536]{1,0:T(8,128)(2,1)S(1)}, f32[1024,1536]{1,0:T(8,128)}) fusion(bf16[512,512]{1,0:T(8,128)(2,1)} %get-tuple-element.20, bf16[512,512]{1,0:T(8,128)(2,1)} %get-tuple-element.21, bf16[512,512]{1,0:T(8,128)(2,1)} %param.21, f32[1024,512]{0,1:T(8,128)} %get-tuple-element.47, f32[512]{0:T(512)S(1)} %bitcast.99, ...), kind=kOutput, calls=%fused_computation.141 | convolution fusion | flops 1619001344 | bytes 13117440 | tf_op jit(solution)/shard_map/dot_general | solution.py:26
  16.5 4.9 %collective-permute-start = (bf16[256,512]{1,0:T(8,128)(2,1)}, bf16[256,512]{1,0:T(8,128)(2,1)S(1)}, u32[]{:S(2)}, u32[]{:S(2)}) collective-permute-start(bf16[256,512]{1,0:T(8,128)(2,1)} %get-tuple-element.22), channel_id=1, source_target_pairs={{0,1},{1,2},{2,3},{3,4},{4,5},{5,6},{6,7},{7,8},{8,9},{9,10},{10,1... | collective-permute-start | bytes 786440 | tf_op jit(solution)/shard_map/ppermute | solution.py:17
  24.0 8.9 %collective-permute-done = bf16[256,512]{1,0:T(8,128)(2,1)S(1)} collective-permute-done((bf16[256,512]{1,0:T(8,128)(2,1)}, bf16[256,512]{1,0:T(8,128)(2,1)S(1)}, u32[]{:S(2)}, u32[]{:S(2)}) %collective-permute-start) | collective-permute-done | bytes 262176 | tf_op jit(solution)/shard_map/ppermute | solution.py:17
  35.7 4.8 %gather_fusion = bf16[1536,512]{1,0:T(8,128)(2,1)S(1)} fusion(bf16[1536,512]{1,0:T(8,128)(2,1)S(1)} %pad_maximum_fusion, s32[2048]{0:T(1024)S(1)} %pad_clamp_fusion), kind=kCustom, calls=%fused_computation | custom fusion | bytes 3151872 | tf_op jit(solution)/shard_map/gather | solution.py:93
  40.5 4.5 %fusion.99 = (f32[1536]{0:T(1024)S(1)}, f32[1536]{0:T(1024)S(1)}, f32[1536,512]{0,1:T(8,128)}) fusion(bf16[5,512,512]{2,1,0:T(8,128)(2,1)} %param.23, bf16[1536,512]{1,0:T(8,128)(2,1)S(1)} %gather_fusion, f32[512]{0:T(512)S(1)} %bitcast.108, bf16[4,1536]{1,0:T(4,128)(2,1)S(1)} %copy-done.18, bf16[3,512,4]{1,2,0:T(4,128)(2,1)S(1)} %copy-done.19), kind=kOutput, calls=%fused_computation.134 | convolution fusion | flops 820245504 | bytes 5273600 | tf_op jit(solution)/shard_map/dot_general | solution.py:26
  45.0 3.4 %fusion.31 = bf16[512,512]{1,0:T(8,128)(2,1)S(1)} fusion(f32[1536,512]{0,1:T(8,128)} %get-tuple-element.50, f32[512]{0:T(512)S(1)} %bitcast.107, f32[1536]{0:T(1024)S(1)} %get-tuple-element.42, f32[1536]{0:T(1024)S(1)} %get-tuple-element.41, s32[1536]{0:T(1024)S(1)} %broadcast_subtract_fusion.1), kind=kOutput, calls=%fused_computation.51 | convolution fusion | flops 810287104 | bytes 3690496 | tf_op jit(solution)/shard_map/dot_general | solution.py:52
  51.4 9.2 %gather_fusion.1 = bf16[2048,512]{1,0:T(8,128)(2,1)} fusion(bf16[512,512]{1,0:T(8,128)(2,1)S(1)} %slice.232, s32[2048]{0:T(1024)S(1)} %broadcast_clamp_fusion), kind=kCustom, calls=%fused_computation.1 | custom fusion | bytes 4202496 | tf_op jit(solution)/shard_map/gather | solution.py:104
  60.6 5.6 %all-to-all-start = ((bf16[32,64,512]{2,1,0:T(8,128)(2,1)}), bf16[32,64,512]{2,1,0:T(8,128)(2,1)S(1)}, u32[]{:S(2)}, u32[]{:S(2)}) async-start(bf16[32,64,512]{2,1,0:T(8,128)(2,1)} %bitcast.96), calls=%async_computation | async-start | bytes 4194304 | tf_op jit(solution)/shard_map/all_to_all | solution.py:105
  66.2 3.1 %slice.166 = f32[1024,512]{1,0:T(8,128)} slice(f32[1024,1536]{1,0:T(8,128)} %get-tuple-element.49), slice={[0:1024], [512:1024]} | slice | bytes 4194304 | tf_op jit(solution)/shard_map/slice | solution.py:87
  69.3 6.2 %broadcast_in_dim.14 = f32[1024,3,512]{2,1,0:T(4,128)} broadcast(f32[1024,512]{1,0:T(8,128)} %slice.166), dimensions={0,2} | broadcast | bytes 8388608 | tf_op jit(solution)/shard_map/broadcast_in_dim | solution.py:129
  75.6 10.8 %reshape.117 = f32[3072,512]{1,0:T(8,128)} reshape(f32[1024,3,512]{2,1,0:T(4,128)} %broadcast_in_dim.14) | data formatting | bytes 12582912 | tf_op jit(solution)/shard_map/reshape | solution.py:129
  87.7 8.9 %gather_fusion.3 = f32[2048,512]{1,0:T(8,128)} fusion(f32[512,512]{1,0:T(8,128)S(1)} %slice.163, s32[2048]{0:T(1024)S(1)} %get-tuple-element.16), kind=kCustom, calls=%fused_computation.3 | custom fusion | bytes 8396800 | tf_op jit(solution)/shard_map/gather | solution.py:111
  99.2 16.9 %all-to-all-done = bf16[32,64,512]{2,1,0:T(8,128)(2,1)S(1)} async-done(((bf16[32,64,512]{2,1,0:T(8,128)(2,1)}), bf16[32,64,512]{2,1,0:T(8,128)(2,1)S(1)}, u32[]{:S(2)}, u32[]{:S(2)}) %all-to-all-start) | async-done | bytes 2097184 | tf_op jit(solution)/shard_map/all_to_all | solution.py:105
  116.1 9.2 %gather_fusion.2 = bf16[2048,512]{1,0:T(8,128)(2,1)} fusion(bf16[2048,512]{1,0:T(8,128)(2,1)S(1)} %bitcast.95, s32[2048]{0:T(1024)S(1)} %fusion.75), kind=kCustom, calls=%fused_computation.2 | custom fusion | bytes 4202496 | tf_op jit(solution)/shard_map/gather | solution.py:110
  125.3 7.3 %fusion.98 = (f32[2048]{0:T(1024)S(1)}, f32[2048]{0:T(1024)S(1)}, f32[2048,512]{0,1:T(8,128)}) fusion(bf16[5,512,512]{2,1,0:T(8,128)(2,1)} %param.23, f32[2048,512]{1,0:T(8,128)} %gather_fusion.3, bf16[2048,512]{1,0:T(8,128)(2,1)} %gather_fusion.2, bf16[4,2048]{1,0:T(4,128)(2,1)S(1)} %copy-done.17, f32[512]{0:T(512)S(1)} %bitcast.106, ...), kind=kOutput, calls=%fused_computation.133 | convolution fusion | flops 1094709248 | bytes 11048960 | tf_op jit(solution)/shard_map/dot_general | solution.py:26
  132.6 4.1 %fusion.34 = bf16[512,512]{1,0:T(8,128)(2,1)S(1)} fusion(f32[2048,512]{0,1:T(8,128)} %get-tuple-element.51, f32[512]{0:T(512)S(1)} %bitcast.105, f32[2048]{0:T(1024)S(1)} %get-tuple-element.40, f32[2048]{0:T(1024)S(1)} %get-tuple-element.39, s32[2048]{0:T(1024)S(1)} %get-tuple-element.17), kind=kOutput, calls=%fused_computation.53 | convolution fusion | flops 1080295424 | bytes 4745216 | tf_op jit(solution)/shard_map/dot_general | solution.py:52
  146.8 5.5 %collective-permute-done.3 = bf16[128,512]{1,0:T(8,128)(2,1)S(1)} collective-permute-done((bf16[128,512]{1,0:T(8,128)(2,1)S(1)}, bf16[128,512]{1,0:T(8,128)(2,1)S(1)}, u32[]{:S(2)}, u32[]{:S(2)}) %collective-permute-start.3) | collective-permute-done | bytes 131104 | tf_op jit(solution)/shard_map/ppermute | solution.py:20
  152.4 13.2 %gather_fusion.4 = bf16[3072,512]{1,0:T(8,128)(2,1)} fusion(bf16[768,512]{1,0:T(8,128)(2,1)S(1)} %pad_maximum_fusion.1, s32[3072]{0:T(1024)S(1)} %fusion.74), kind=kCustom, calls=%fused_computation.4 | custom fusion | bytes 6303744 | tf_op jit(solution)/shard_map/gather | solution.py:133
  165.7 8.3 %fusion.97 = (f32[3072]{0:T(1024)S(1)}, f32[3072]{0:T(1024)S(1)}, f32[3072,512]{1,0:T(8,128)}) fusion(bf16[5,512,512]{2,1,0:T(8,128)(2,1)} %param.23, f32[3072,512]{1,0:T(8,128)} %reshape.117, bf16[3072,512]{1,0:T(8,128)(2,1)} %gather_fusion.4, f32[512]{0:T(512)S(1)} %bitcast.103, bf16[4,3072]{1,0:T(4,128)(2,1)S(1)} %copy-done.16, ...), kind=kOutput, calls=%fused_computation.132 | convolution fusion | flops 1642063872 | bytes 16308224 | tf_op jit(solution)/shard_map/dot_general | solution.py:26
  173.9 3.7 %multiply_convert_fusion = bf16[3072,512]{1,0:T(8,128)(2,1)S(1)} fusion(f32[3072,512]{1,0:T(8,128)} %get-tuple-element.53, f32[512]{0:T(512)S(1)} %bitcast.100, f32[3072]{0:T(1024)S(1)} %get-tuple-element.38, f32[3072]{0:T(1024)S(1)} %get-tuple-element.37), kind=kLoop, calls=%fused_computation.5 | loop fusion | flops 6291456 | bytes 9463808 | tf_op jit(solution)/shard_map/convert_element_type | solution.py:45
  177.7 4.3 %reshape.118 = bf16[1024,3,512]{2,1,0:T(4,128)(2,1)} reshape(bf16[3072,512]{1,0:T(8,128)(2,1)S(1)} %multiply_convert_fusion) | data formatting | bytes 6291456 | tf_op jit(solution)/shard_map/reshape | solution.py:140
  182.0 7.3 %reduce = bf16[1024,512]{1,0:T(8,128)(2,1)S(1)} reduce(bf16[1024,3,512]{2,1,0:T(4,128)(2,1)} %reshape.118, bf16[]{:T(256)} %constant.67), dimensions={1}, to_apply=%region_10.11.clone | reduce | flops 1048576 | bytes 4194306 | tf_op jit(solution)/shard_map/reduce_sum | solution.py:140
  189.3 4.1 %fusion.30 = f32[227,1024]{1,0:T(8,128)} fusion(bf16[227,512]{1,0:T(8,128)(2,1)S(1)} %copy-done.15, f32[1024,1536]{1,0:T(8,128)} %get-tuple-element.49, bf16[1024,512]{1,0:T(8,128)(2,1)S(1)} %reduce, f32[512]{0:T(512)S(1)} %bitcast.102, bf16[4,2,512,512]{3,2,1,0:T(8,128)(2,1)} %param.22, f32[227]{0:T(256)S(1)} %copy-done.20), kind=kOutput, calls=%fused_computation.50 | convolution fusion | flops 778800128 | bytes 4835212 | tf_op jit(solution)/shard_map/dot_general | solution.py:26
  (78 shorter events, 27.9 us)
Async XLA Ops:
  0.6 4.8 %copy-start = (bf16[227,1024]{1,0:T(8,128)(2,1)S(1)}, bf16[227,1024]{1,0:T(8,128)(2,1)}, u32[]{:S(2)}) copy-start(bf16[227,1024]{1,0:T(8,128)(2,1)} %param.19) | copy-start | bytes 1394692
  0.6 4.8 %copy-start.14 = (bf16[512,227]{0,1:T(8,128)(2,1)S(1)}, bf16[512,227]{0,1:T(8,128)(2,1)}, u32[]{:S(2)}) copy-start(bf16[512,227]{0,1:T(8,128)(2,1)} %param.20) | copy-start | bytes 697348
  9.0 13.8 %copy-start.8 = (s32[32,64]{1,0:T(8,128)S(1)}, s32[32,64]{1,0:T(8,128)}, u32[]{:S(2)}) copy-start(s32[32,64]{1,0:T(8,128)} %param.36) | copy-start | bytes 24580
  9.0 13.9 %copy-start.11 = (s32[1536]{0:T(1024)S(1)}, s32[1536]{0:T(1024)}, u32[]{:S(2)}) copy-start(s32[1536]{0:T(1024)} %param.32) | copy-start | bytes 18436
  15.7 8.3 %copy-start.12 = (s32[1536]{0:T(1024)S(1)}, s32[1536]{0:T(1024)}, u32[]{:S(2)}) copy-start(s32[1536]{0:T(1024)} %param.33) | copy-start | bytes 18436
  16.5 16.4 %collective-permute-start = (bf16[256,512]{1,0:T(8,128)(2,1)}, bf16[256,512]{1,0:T(8,128)(2,1)S(1)}, u32[]{:S(2)}, u32[]{:S(2)}) collective-permute-start(bf16[256,512]{1,0:T(8,128)(2,1)} %get-tuple-element.22), channel_id=1, source_target_pairs={{0,1},{1,2},{2,3},{3,4},{4,5},{5,6},{6,7},{7,8},{8,9},{9,10},{10,1... | collective-permute-start | bytes 786440 | tf_op jit(solution)/shard_map/ppermute | solution.py:17
  21.5 12.8 %collective-permute-start.1 = (bf16[256,512]{1,0:T(8,128)(2,1)}, bf16[256,512]{1,0:T(8,128)(2,1)}, u32[]{:S(2)}, u32[]{:S(2)}) collective-permute-start(bf16[256,512]{1,0:T(8,128)(2,1)} %get-tuple-element.23), channel_id=1, source_target_pairs={{1,0},{2,1},{3,2},{4,3},{5,4},{6,5},{7,6},{8,7},{9,8},{10,9},{11,1... | collective-permute-start | bytes 786440 | tf_op jit(solution)/shard_map/ppermute | solution.py:20
  35.7 4.8 %copy-start.18 = (bf16[4,1536]{1,0:T(4,128)(2,1)S(1)}, bf16[4,1536]{1,0:T(4,128)(2,1)}, u32[]{:S(2)}) copy-start(bf16[4,1536]{1,0:T(4,128)(2,1)} %param.29) | copy-start | bytes 36868
  35.7 4.8 %copy-start.19 = (bf16[3,512,4]{1,2,0:T(4,128)(2,1)S(1)}, bf16[3,512,4]{1,2,0:T(4,128)(2,1)}, u32[]{:S(2)}) copy-start(bf16[3,512,4]{1,2,0:T(4,128)(2,1)} %param.26) | copy-start | bytes 36868
  45.0 4.3 %copy-start.5 = (bf16[512,512]{1,0:T(8,128)(2,1)S(1)}, bf16[512,512]{1,0:T(8,128)(2,1)}, u32[]{:S(2)}) copy-start(bf16[512,512]{1,0:T(8,128)(2,1)} %get-tuple-element.18) | copy-start | bytes 1572868
  45.0 4.2 %copy-start.6 = (bf16[512,512]{1,0:T(8,128)(2,1)S(1)}, bf16[512,512]{1,0:T(8,128)(2,1)}, u32[]{:S(2)}) copy-start(bf16[512,512]{1,0:T(8,128)(2,1)} %get-tuple-element.19) | copy-start | bytes 1572868
  60.6 55.5 %all-to-all-start = ((bf16[32,64,512]{2,1,0:T(8,128)(2,1)}), bf16[32,64,512]{2,1,0:T(8,128)(2,1)S(1)}, u32[]{:S(2)}, u32[]{:S(2)}) async-start(bf16[32,64,512]{2,1,0:T(8,128)(2,1)} %bitcast.96), calls=%async_computation | async-start | bytes 4194304 | tf_op jit(solution)/shard_map/all_to_all | solution.py:105
  75.6 10.8 %copy-start.13 = (s32[2048]{0:T(1024)S(1)}, s32[2048]{0:T(1024)}, u32[]{:S(2)}) copy-start(s32[2048]{0:T(1024)} %param.35) | copy-start | bytes 24580
  75.6 10.8 %copy-start.10 = (s32[2048]{0:T(1024)S(1)}, s32[2048]{0:T(1024)}, u32[]{:S(2)}) copy-start(s32[2048]{0:T(1024)} %param.34) | copy-start | bytes 24580
  116.1 9.2 %copy-start.17 = (bf16[4,2048]{1,0:T(4,128)(2,1)S(1)}, bf16[4,2048]{1,0:T(4,128)(2,1)}, u32[]{:S(2)}) copy-start(bf16[4,2048]{1,0:T(4,128)(2,1)} %param.30) | copy-start | bytes 49156
  132.6 4.1 %copy-start.7 = (f32[512,512]{1,0:T(8,128)S(1)}, f32[512,512]{1,0:T(8,128)}, u32[]{:S(2)}) copy-start(f32[512,512]{1,0:T(8,128)} %fusion.57) | copy-start | bytes 3145732
  136.7 2.7 %copy-start.4 = (bf16[512,512]{1,0:T(8,128)(2,1)S(1)}, bf16[512,512]{1,0:T(8,128)(2,1)}, u32[]{:S(2)}) copy-start(bf16[512,512]{1,0:T(8,128)(2,1)} %copy-done.3) | copy-start | bytes 1572868
  139.0 5.8 %copy-start.9 = (s32[3072]{0:T(1024)S(1)}, s32[3072]{0:T(1024)}, u32[]{:S(2)}) copy-start(s32[3072]{0:T(1024)} %param.37) | copy-start | bytes 36868
  141.2 5.6 %collective-permute-start.2 = (bf16[128,512]{1,0:T(8,128)(2,1)S(1)}, bf16[128,512]{1,0:T(8,128)(2,1)S(1)}, u32[]{:S(2)}, u32[]{:S(2)}) collective-permute-start(bf16[128,512]{1,0:T(8,128)(2,1)S(1)} %get-tuple-element.24), channel_id=1, source_target_pairs={{0,1},{1,2},{2,3},{3,4},{4,5},{5,6},{6,7},{7,8},{8,9},{9,10},{10,1... | collective-permute-start | bytes 393224 | tf_op jit(solution)/shard_map/ppermute | solution.py:17
  143.3 9.1 %collective-permute-start.3 = (bf16[128,512]{1,0:T(8,128)(2,1)S(1)}, bf16[128,512]{1,0:T(8,128)(2,1)S(1)}, u32[]{:S(2)}, u32[]{:S(2)}) collective-permute-start(bf16[128,512]{1,0:T(8,128)(2,1)S(1)} %get-tuple-element.25), channel_id=1, source_target_pairs={{1,0},{2,1},{3,2},{4,3},{5,4},{6,5},{7,6},{8,7},{9,8},{10,9},{11,1... | collective-permute-start | bytes 393224 | tf_op jit(solution)/shard_map/ppermute | solution.py:20
  152.4 13.2 %copy-start.16 = (bf16[4,3072]{1,0:T(4,128)(2,1)S(1)}, bf16[4,3072]{1,0:T(4,128)(2,1)}, u32[]{:S(2)}) copy-start(bf16[4,3072]{1,0:T(4,128)(2,1)} %param.31) | copy-start | bytes 73732
  182.0 7.3 %copy-start.15 = (bf16[227,512]{1,0:T(8,128)(2,1)S(1)}, bf16[227,512]{1,0:T(8,128)(2,1)}, u32[]{:S(2)}) copy-start(bf16[227,512]{1,0:T(8,128)(2,1)} %param.27) | copy-start | bytes 697348
  182.0 7.3 %copy-start.20 = (f32[227]{0:T(256)S(1)}, f32[227]{0:T(256)}, u32[]{:S(2)}) copy-start(f32[227]{0:T(256)} %param.28) | copy-start | bytes 2728
  189.3 4.1 %copy-start.1 = (bf16[227,1024]{1,0:T(8,128)(2,1)S(1)}, bf16[227,1024]{1,0:T(8,128)(2,1)}, u32[]{:S(2)}) copy-start(bf16[227,1024]{1,0:T(8,128)(2,1)} %param.19) | copy-start | bytes 1394692
  (2 other events, 2.2 us)
where the time goes:
time: 194 us; the launch traced here: 193 us
  local copies, waits for them, and re-layouts  81.4 us (42%)
  matrix products  49.1 us (25%)
  waiting for transfers between devices  33.6 us (17%)
  starting transfers between devices  15.4 us (8%)
  other arithmetic  12.8 us (7%)
    dot_general x10, matrix products, by_rows(): lax.dot_general(values, weight, (((1,), (1,)), ((), ())), preferred_eleme...  41.7 us
    all_to_all x1, waiting for transfers between devices, body(): lax.all_to_all(outgoing, ('space', 'chan'), split_axis=0, concat_axis=0,...  16.9 us
    gather x1, local copies, waits for them, and re-layouts, body(): widened[mesh_sender].astype(jnp.float32) + expanded  13.2 us
    reshape x1, local copies, waits for them, and re-layouts, body(): jnp.broadcast_to(decode_grid[:, None, :], (grid_cells, 3, width))  10.8 us
    ppermute x2, waiting for transfers between devices, padded(): lax.ppermute(lax.slice_in_dim(block, block.shape[dim] - width, None, axis...  9.93 us
    gather x1, local copies, waits for them, and re-layouts, body(): link_send[mesh_rows.reshape(-1)]  9.17 us
    gather x1, local copies, waits for them, and re-layouts, body(): arrived[mesh_slot].astype(jnp.float32) + link_recv[recv_local]  9.17 us
    gather x1, local copies, waits for them, and re-layouts, body(): link_recv[recv_local]  8.88 us
  transfers between devices with their start and end apart: 5, of which 5 were waited for; matrix products, arithmetic and copies ran while one was open for 18% of the time, Pallas kernels for 0%

commit v1 on v0

v1 whole, which is shorter than its diff:
```python
import functools

import jax
import jax.numpy as jnp
from jax import lax
from jax.experimental import pallas as pl
from jax.experimental.pallas import tpu as pltpu
from jax.sharding import PartitionSpec as P

M_DEV = 512
BLOCK = 256

eps = 1e-05
bf16 = jnp.bfloat16
f32 = jnp.float32


def contract(left, right, left_dim, right_dim):
    return lax.dot_general(
        left, right, (((left_dim,), (right_dim,)), ((), ())), preferred_element_type=f32
    )


def nn(left, right):
    return contract(left, right, 1, 0)


def nt(left, right):
    return contract(left, right, 1, 1)


def tn(left, right):
    return contract(left, right, 0, 0)


def swish(values):
    half = values * 0.5
    return half * jnp.tanh(half) + half


def norm_columns(values, gain):
    count = 1.0 / values.shape[0]
    mean = jnp.sum(values, axis=0, keepdims=True) * count
    var = jnp.sum(values * values, axis=0, keepdims=True) * count - mean * mean
    return (values - mean) * lax.rsqrt(var + eps) * gain


def pick_rows(index_row, count):
    rows = lax.broadcasted_iota(jnp.int32, (count, index_row.shape[1]), 0)
    return jnp.where(rows == index_row, 1.0, 0.0).astype(bf16)


def pick_columns(index_column, count):
    columns = lax.broadcasted_iota(jnp.int32, (index_column.shape[0], count), 1)
    return jnp.where(columns == index_column, 1.0, 0.0).astype(bf16)


def blocks(total):
    return [pl.ds(start, BLOCK) for start in range(0, total, BLOCK)]


def embed_columns(x, embed_w, second_w, bias, gain):
    hidden = swish(nn(embed_w, x) + bias).astype(bf16)
    return norm_columns(nn(second_w, hidden), gain).astype(bf16)


def embed_kernel(x, embed_w, second_w, send_w, bias, gain, latent, send):
    for part in blocks(x.shape[1]):
        cells = embed_columns(x[:, part], embed_w[...], second_w[...], bias[...], gain[...])
        latent[:, part] = cells
        send[:, part] = nn(send_w[...], cells).astype(bf16)


def encode_kernel(
    own,
    low,
    high,
    embed_w,
    embed_second_w,
    send_w,
    embed_bias,
    embed_gain,
    geom,
    geom_w,
    send_index,
    recv_index,
    edge_w,
    edge_gain,
    link_w,
    slot_rows,
    latent,
    outgoing,
    table,
    picks,
    messages,
    sums,
):
    reach = low.shape[1]
    cells = own.shape[1]
    edges = geom.shape[1]
    ext = cells + 2 * reach
    width = own.shape[0]
    table[:, reach : reach + cells] = own[...]
    for start, halo in ((0, low), (reach + cells, high)):
        values = embed_columns(
            halo[...], embed_w[...], embed_second_w[...], embed_bias[...], embed_gain[...]
        )
        table[:, start : start + reach] = nn(send_w[...], values).astype(bf16)
    table[:, ext:] = geom_w[...]
    for part in blocks(edges):
        picks[:ext, :] = pick_rows(send_index[:, part], ext)
        picks[ext:, :] = geom[:, part]
        hidden = swish(nn(table[...], picks[...])).astype(bf16)
        messages[:, part] = norm_columns(nn(edge_w[...], hidden), edge_gain[...]).astype(bf16)
        sums[:, part] = pick_rows(recv_index[:, part], sums.shape[0])
    nodes = nt(sums[...], messages[...]).astype(bf16)
    latent[...] = nodes
    link = nt(nodes, link_w[...]).astype(bf16)
    for part in blocks(outgoing.shape[0]):
        outgoing[part, :] = nn(pick_columns(slot_rows[part, :], width), link).astype(bf16)


def window_kernel(
    latent,
    recv_column,
    recv_w,
    mesh_geom,
    mesh_geom_w,
    node_w,
    node_bias,
    grid_latent,
    decode_w,
    out_w,
    out_bias,
    cell_geom,
    cell_geom_w,
    recv_terms,
    node_terms,
    latent_columns,
    cell_terms,
    out_terms,
):
    nodes = latent[...]
    for part in blocks(recv_terms.shape[0]):
        picked = nn(pick_columns(recv_column[part, :], nodes.shape[0]), nodes).astype(bf16)
        recv_terms[part, :] = nt(picked, recv_w[...]) + tn(mesh_geom[:, part], mesh_geom_w[...])
    node_terms[...] = nt(node_w[...], nodes) + node_bias[...]
    latent_columns[...] = jnp.transpose(nodes.astype(f32))
    for part in blocks(grid_latent.shape[1]):
        cells = grid_latent[:, part]
        out_terms[:, part] = nn(out_w[...], cells) + out_bias[...]
        terms = nn(decode_w[...], cells)
        for k in range(cell_terms.shape[0]):
            cell_terms[k, :, part] = terms + nn(cell_geom_w[...], cell_geom[k, :, part])


def mesh_kernel(
    arrived,
    slot_column,
    recv_terms,
    recv_index,
    edge_w,
    edge_gain,
    node_terms,
    node_w,
    node_second_w,
    node_gain,
    latent_columns,
    send_w,
    state,
    send,
    send_low,
    send_high,
    messages,
    sums,
):
    reach = send_low.shape[1]
    for part in blocks(recv_terms.shape[0]):
        picks = pick_columns(slot_column[part, :], arrived.shape[0])
        hidden = swish(nn(picks, arrived[...]) + recv_terms[part, :]).astype(bf16)
        messages[:, part] = norm_columns(nt(edge_w[...], hidden), edge_gain[...]).astype(bf16)
        sums[:, part] = pick_rows(recv_index[:, part], sums.shape[0])
    nodes = nt(sums[...], messages[...]).astype(bf16)
    hidden = swish(nt(node_w[...], nodes) + node_terms[...]).astype(bf16)
    values = latent_columns[...] + norm_columns(nn(node_second_w[...], hidden), node_gain[...])
    values = values.astype(bf16)
    state[...] = values
    sent = nn(send_w[...], values).astype(bf16)
    send[...] = sent
    send_low[...] = sent[:, :reach]
    send_high[...] = sent[:, sent.shape[1] - reach :]


def local_kernel(send, index, terms, out):
    for k in range(terms.shape[0]):
        out[k] = terms[k] + nn(send[...], pick_rows(index[k], send.shape[1]))


def decode_kernel(
    low, high, index, terms, edge_w, edge_gain, out_terms, gathered_w, out_w, out_bias, prediction
):
    reach = low.shape[1]
    halo = jnp.concatenate([low[...], high[...]], axis=1)
    total = None
    for k in range(terms.shape[0]):
        hidden = swish(terms[k] + nn(halo, pick_rows(index[k], 2 * reach))).astype(bf16)
        message = norm_columns(nn(edge_w[...], hidden), edge_gain[...]).astype(bf16).astype(f32)
        total = message if total is None else total + message
    hidden = swish(out_terms[...] + nn(gathered_w[...], total.astype(bf16))).astype(bf16)
    prediction[...] = nn(out_w[...], hidden) + out_bias[...]


def call(kernel, outs, *args, scratch=()):
    return pl.pallas_call(
        kernel,
        out_shape=outs,
        scratch_shapes=scratch,
        compiler_params=pltpu.CompilerParams(vmem_limit_bytes=56 << 20),
    )(*args)


def split_bias(bias):
    high = bias.astype(bf16)
    rest = bias - high.astype(f32)
    middle = rest.astype(bf16)
    low = (rest - middle.astype(f32)).astype(bf16)
    return jnp.stack([high, middle, low], axis=-1)


def exchange(low_end, high_end):
    axes = ("space", "chan")
    count = lax.axis_size("space") * lax.axis_size("chan")
    up = [(i, (i + 1) % count) for i in range(count)]
    down = [(target, source) for source, target in up]
    return lax.ppermute(high_end, axes, up), lax.ppermute(low_end, axes, down)


def body(
    grid_in,
    grid_embed_w,
    g2m_w,
    pair_w,
    second_w,
    first_b,
    norm_gain,
    geom_w,
    out_w,
    out_b,
    g2m_geom,
    mesh_geom,
    m2g_geom,
    g2m_send,
    g2m_recv,
    mesh_recv,
    mesh_slot,
    mesh_rows,
    m2g_send,
):
    width = grid_embed_w.shape[0]
    cells = grid_in.shape[1]
    position = lax.axis_index(("space", "chan"))
    reach = cells // 4
    low, high = exchange(grid_in[:, :reach], grid_in[:, cells - reach :])

    bias_columns = first_b.T
    gain_columns = norm_gain.T
    bias = lambda i: bias_columns[:, i : i + 1]
    gain = lambda i: gain_columns[:, i : i + 1]
    shape = jax.ShapeDtypeStruct

    def geom_weights(i, bias_index, pad):
        weights = jnp.concatenate([geom_w[i], split_bias(first_b[bias_index])], axis=1)
        return jnp.pad(weights, ((0, 0), (0, pad - weights.shape[1])))

    def geom_rows(values, pad):
        lead = values.shape[:-2]
        edges = values.shape[-1]
        used = values.shape[-2] + 3
        return jnp.concatenate(
            [values, jnp.ones(lead + (3, edges), bf16), jnp.zeros(lead + (pad - used, edges), bf16)],
            axis=-2,
        )

    grid_latent, own_send = call(
        embed_kernel,
        (shape((width, cells), bf16), shape((width, cells), bf16)),
        grid_in,
        grid_embed_w,
        second_w[0],
        g2m_w,
        bias(0),
        gain(0),
    )

    edges = g2m_geom.shape[1]
    pad = 128
    ext = cells + 2 * reach
    slots = mesh_rows.size
    latent, outgoing = call(
        encode_kernel,
        (shape((M_DEV, width), bf16), shape((slots, width), bf16)),
        own_send,
        low,
        high,
        grid_embed_w,
        second_w[0],
        g2m_w,
        bias(0),
        gain(0),
        geom_rows(g2m_geom, pad),
        geom_weights(0, 1, pad),
        (g2m_send - position * cells + reach)[None, :],
        (g2m_recv - position * M_DEV)[None, :],
        second_w[1],
        gain(1),
        pair_w[0, 0],
        mesh_rows.reshape(-1, 1),
        scratch=[
            pltpu.VMEM((width, ext + pad), bf16),
            pltpu.VMEM((ext + pad, BLOCK), bf16),
            pltpu.VMEM((width, edges), bf16),
            pltpu.VMEM((M_DEV, edges), bf16),
        ],
    )
    arrived = lax.all_to_all(
        outgoing.reshape(mesh_rows.shape + (width,)),
        ("space", "chan"),
        split_axis=0,
        concat_axis=0,
        tiled=True,
    ).reshape(-1, width)

    mesh_edges = mesh_geom.shape[1]
    recv_local = mesh_recv - position * M_DEV
    per_cell = m2g_send.shape[0] // cells
    cell_geom = m2g_geom.reshape(-1, cells, per_cell).transpose(2, 0, 1)
    recv_terms, node_terms, latent_columns, cell_terms, out_terms = call(
        window_kernel,
        (
            shape((mesh_edges, width), f32),
            shape((width, M_DEV), f32),
            shape((width, M_DEV), f32),
            shape((per_cell, width, cells), f32),
            shape((width, cells), f32),
        ),
        latent,
        recv_local.reshape(-1, 1),
        pair_w[0, 1],
        geom_rows(mesh_geom, 8),
        geom_weights(1, 2, 8).T,
        pair_w[1, 0],
        bias(3),
        grid_latent,
        pair_w[2, 1],
        pair_w[3, 0],
        bias(5),
        geom_rows(cell_geom, 8),
        geom_weights(2, 4, 8),
    )

    mesh_reach = M_DEV // 4
    state, send, send_low, send_high = call(
        mesh_kernel,
        (
            shape((width, M_DEV), bf16),
            shape((width, M_DEV), bf16),
            shape((width, mesh_reach), bf16),
            shape((width, mesh_reach), bf16),
        ),
        arrived,
        mesh_slot.reshape(-1, 1),
        recv_terms,
        recv_local[None, :],
        second_w[2],
        gain(2),
        node_terms,
        pair_w[1, 1],
        second_w[3],
        gain(3),
        latent_columns,
        pair_w[2, 0],
        scratch=[
            pltpu.VMEM((width, mesh_edges), bf16),
            pltpu.VMEM((M_DEV, mesh_edges), bf16),
        ],
    )
    low, high = exchange(send_low, send_high)

    own_index = (m2g_send - position * M_DEV).reshape(cells, per_cell).T[:, None, :]
    halo_index = jnp.where(
        own_index < 0,
        own_index + mesh_reach,
        jnp.where(own_index >= M_DEV, own_index - M_DEV + mesh_reach, -1),
    )
    whole = lambda *dims: pl.BlockSpec(dims, lambda i: (0,) * len(dims))
    index_spec = pl.BlockSpec((per_cell, 1, BLOCK), lambda i: (0, 0, i))
    terms_spec = pl.BlockSpec((per_cell, width, BLOCK), lambda i: (0, 0, i))
    params = pltpu.CompilerParams(vmem_limit_bytes=56 << 20)
    cell_terms = pl.pallas_call(
        local_kernel,
        grid=(cells // BLOCK,),
        in_specs=[whole(width, M_DEV), index_spec, terms_spec],
        out_specs=terms_spec,
        out_shape=shape(cell_terms.shape, f32),
        compiler_params=params,
    )(send, own_index, cell_terms)
    channels = out_w.shape[0]
    prediction = pl.pallas_call(
        decode_kernel,
        grid=(cells // BLOCK,),
        in_specs=[
            whole(width, mesh_reach),
            whole(width, mesh_reach),
            index_spec,
            terms_spec,
            whole(width, width),
            whole(width, 1),
            pl.BlockSpec((width, BLOCK), lambda i: (0, i)),
            whole(width, width),
            whole(channels, width),
            whole(channels, 1),
        ],
        out_specs=pl.BlockSpec((channels, BLOCK), lambda i: (0, i)),
        out_shape=shape((channels, cells), f32),
        compiler_params=params,
    )(
        low,
        high,
        halo_index,
        cell_terms,
        second_w[4],
        gain(4),
        out_terms,
        pair_w[3, 1],
        out_w,
        out_b[:, None],
    )
    return (prediction, state)


def solution(mesh):
    split = ("space", "chan")
    return jax.shard_map(
        body,
        mesh=mesh,
        in_specs=(
            P(None, split),
            P(),
            P(),
            P(),
            P(),
            P(),
            P(),
            P(),
            P(),
            P(),
            P(None, split),
            P(None, split),
            P(None, split),
            P(split),
            P(split),
            P(split),
            P(split),
            P(split, None),
            P(split),
        ),
        out_specs=(P(None, split), P(None, split)),
        check_vma=False,
    )
```

time: 194 us -> 147 us (0.76)
  Pallas kernels: 0 us -> 66.8 us
  local copies, waits for them, and re-layouts: 81.4 us -> 30.2 us
  matrix products: 49.1 us -> 0 us
  other arithmetic: 12.8 us -> 3.73 us
  waiting for transfers between devices: 33.6 us -> 29.6 us
    pallas_call x0 -> x6, Pallas kernels: none -> 66.8 us  [the longest x4 48.3 us: call(): pl.pallas_call(kernel, out_shape=outs, scratch_shapes=scratch, compiler_p...]
    dot_general x12 -> x0, matrix products: 49.1 us -> none  [the longest x10 41.7 us: by_rows(): lax.dot_general(values, weight, (((1,), (1,)), ((), ())), preferred_eleme...]
    gather x5 -> x0, local copies, waits for them, and re-layouts: 45.3 us -> none  [the longest x1 13.2 us: body(): widened[mesh_sender].astype(jnp.float32) + expanded]
    ppermute x4, waiting for transfers between devices: 16.8 us -> 0.01 us  [exchange(): return (lax.ppermute(high_end, axes, up), lax.ppermute(low_end, axes, down))]
    all_to_all x1, waiting for transfers between devices: 16.9 us -> 29.6 us  [body(): lax.all_to_all(outgoing.reshape(mesh_rows.shape + (width,)), ('space', 'c...]
    reshape x3 -> x7, local copies, waits for them, and re-layouts: 15.2 us -> 7.83 us  [the longest x2 2.56 us: body(): cell_geom = m2g_geom.reshape(-1, cells, per_cell).transpose(2, 0, 1)]
    reduce_sum x1 -> x0, other arithmetic: 7.28 us -> none  [body(): message.astype(jnp.float32).reshape(grid_cells, 3, width).sum(axis=1)]
    slice x8 -> x2, local copies, waits for them, and re-layouts: 8.2 us -> 2.78 us  [the longest x1 1.77 us: body(): gain = lambda i: gain_columns[:, i:i + 1]]
  transfers between devices with their start and end apart: 5 -> 5, of which waited for: 5 -> 1; matrix products, arithmetic and copies ran while one was open for 18% -> 21% of each run, Pallas kernels for 0% -> 16%
where the time goes in v1:
time: 147 us; the launch traced here: 146 us
  Pallas kernels  66.8 us (45%)
  local copies, waits for them, and re-layouts  30.2 us (21%)
  waiting for transfers between devices  29.6 us (20%)
  starting transfers between devices  14.8 us (10%)
  other arithmetic  3.73 us (3%)
    pallas_call x4, Pallas kernels, call(): pl.pallas_call(kernel, out_shape=outs, scratch_shapes=scratch, compiler_p...  48.3 us
    all_to_all x1, waiting for transfers between devices, body(): lax.all_to_all(outgoing.reshape(mesh_rows.shape + (width,)), ('space', 'c...  29.6 us
    ppermute x4, starting transfers between devices, exchange(): return (lax.ppermute(high_end, axes, up), lax.ppermute(low_end, axes, down))  11.9 us
    pallas_call x1, Pallas kernels, body(): pl.pallas_call(decode_kernel, grid=(cells // BLOCK,), in_specs=[whole(wid...  11.5 us
    pallas_call x1, Pallas kernels, body(): pl.pallas_call(local_kernel, grid=(cells // BLOCK,), in_specs=[whole(widt...  7.09 us
    unnamed x37, local copies, waits for them, and re-layouts  5.33 us
    squeeze x1, local copies, waits for them, and re-layouts, body(): pair_w[3, 1]  4.17 us
    squeeze x1, local copies, waits for them, and re-layouts, body(): second_w[4]  3.23 us
  transfers between devices with their start and end apart: 5, of which 1 were waited for; matrix products, arithmetic and copies ran while one was open for 21% of the time, Pallas kernels for 16%

profile of v1, /device:TPU:0, one launch (start us, length us, event | category | flops | bytes accessed | tf_op | source)
XLA Modules:
  0.0 145.9 jit_solution(8682652059027299376)
XLA Ops:
  0.6 1.0 fusion.13
  1.7 3.1 %collective-permute-start = (bf16[227,256]{1,0:T(8,128)(2,1)S(1)}, bf16[227,256]{1,0:T(8,128)(2,1)S(1)}, u32[]{:S(2)}, u32[]{:S(2)}) collective-permute-start(bf16[227,256]{1,0:T(8,128)(2,1)S(1)} %get-tuple-element.42), channel_id=1, source_target_pairs={{0,1},{1,2},{2,3},{3,4},{4,5},{5,6},{6,7},{7,8},{8,9},{9,10},{10,1... | collective-permute-start | bytes 348680 | tf_op jit(solution)/shard_map/ppermute | solution.py:235
  4.7 3.5 %collective-permute-start.1 = (bf16[227,256]{1,0:T(8,128)(2,1)S(1)}, bf16[227,256]{1,0:T(8,128)(2,1)S(1)}, u32[]{:S(2)}, u32[]{:S(2)}) collective-permute-start(bf16[227,256]{1,0:T(8,128)(2,1)S(1)} %get-tuple-element.41), channel_id=1, source_target_pairs={{1,0},{2,1},{3,2},{4,3},{5,4},{6,5},{7,6},{8,7},{9,8},{10,9},{11,1... | collective-permute-start | bytes 348680 | tf_op jit(solution)/shard_map/ppermute | solution.py:235
  8.2 0.8 fusion.12
  9.9 0.9 copy.45
  11.7 0.9 copy.46
  12.5 3.2 %slice_bitcast_fusion.1 = (bf16[512,512]{1,0:T(8,128)(2,1)}, bf16[512,512]{1,0:T(8,128)(2,1)}, bf16[512,512]{1,0:T(8,128)(2,1)}, bf16[512,512]{1,0:T(8,128)(2,1)}, bf16[512,512]{1,0:T(8,128)(2,1)}) fusion(bf16[5,512,512]{2,1,0:T(8,128)(2,1)} %param.23), kind=kLoop, calls=%fused_computation.1 | loop fusion | bytes 5242880 | tf_op jit(solution)/shard_map/squeeze | solution.py:431
  16.6 4.2 %slice_bitcast_fusion = (bf16[512,512]{1,0:T(8,128)(2,1)}, bf16[512,512]{1,0:T(8,128)(2,1)}, bf16[512,512]{1,0:T(8,128)(2,1)}, bf16[512,512]{1,0:T(8,128)(2,1)},...) fusion(bf16[4,2,512,512]{3,2,1,0:T(8,128)(2,1)} %param.22), kind=kLoop, calls=%fused_computation | loop fusion | bytes 8388608 | tf_op jit(solution)/shard_map/squeeze | solution.py:434
  22.3 1.8 %fusion.14 = (f32[512,1]{1,0:T(8,128)}, f32[512,1]{1,0:T(8,128)}, f32[512,1]{1,0:T(8,128)}, f32[512,1]{1,0:T(8,128)}, f32[512,1]{1,0:T(8,128)}, /*index=5*/f32[512,1]{1,0:T(8,128)}, f32[512,1]{1,0:T(8,128)}, f32[512,1]{1,0:T(8,128)}) fusion(f32[512,5]{1,0:T(8,128)S(1)} %bitcast.95, f32[512,6]{1,0:T(8,128)S(1)} %bitcast.97), kind=kLoop, calls=%fused_computation.53 | loop fusion | bytes 32768 | tf_op jit(solution)/shard_map/slice | solution.py:268
  24.0 0.8 maximum_maximum_fusion.geom
  25.5 2.0 %reshape.174.slot_rows = s32[2048,1]{1,0:T(8,128)} reshape(s32[32,64]{1,0:T(8,128)S(1)} %copy-done.8) | data formatting | bytes 16384 | tf_op jit(solution)/shard_map/reshape | solution.py:317
  27.5 6.0 %shard_map.194 = (bf16[512,1024]{1,0:T(8,128)(2,1)}, bf16[512,1024]{1,0:T(8,128)(2,1)}) custom-call(bf16[227,1024]{1,0:T(8,128)(2,1)} %x.7, bf16[512,227]{1,0:T(8,128)(2,1)} %copy.47.embed_w, bf16[512,512]{1,0:T(8,128)(2,1)} %get-tuple-element.39.second_w.embed_second_w, bf16[512,512]{1,0:T(8,128)(2,1)} %send_w.3, ...), custom_call_target="tpu_custom_call" | custom-call | tf_op jit(solution)/shard_map/pallas_call | solution.py:214
  34.2 15.8 %shard_map.195 = (bf16[512,512]{1,0:T(8,128)(2,1)}, bf16[2048,512]{1,0:T(8,128)(2,1)}) custom-call(bf16[512,1024]{1,0:T(8,128)(2,1)} %get-tuple-element.15.own, bf16[227,256]{1,0:T(8,128)(2,1)} %copy-done.4, bf16[227,256]{1,0:T(8,128)(2,1)} %copy-done.5, bf16[512,227]{1,0:T(8,128)(2,1)} %copy.47.embed_w, ...), custom_call_target="tpu_custom_call" | custom-call | tf_op jit(solution)/shard_map/pallas_call | solution.py:214
  50.0 2.9 %all-to-all-start = ((bf16[32,64,512]{2,1,0:T(8,128)(2,1)}), bf16[32,64,512]{2,1,0:T(8,128)(2,1)S(1)}, u32[]{:S(2)}, u32[]{:S(2)}) async-start(bf16[32,64,512]{2,1,0:T(8,128)(2,1)} %bitcast.98), calls=%async_computation | async-start | bytes 4194304 | tf_op jit(solution)/shard_map/all_to_all | solution.py:325
  53.9 1.4 copy.53.recv_column
  55.3 2.2 %reshape.172 = bf16[4,1024,3]{2,1,0:T(8,128)(2,1)S(1)} reshape(bf16[4,3072]{1,0:T(4,128)(2,1)S(1)} %copy-done.7) | data formatting | bytes 49152 | tf_op jit(solution)/shard_map/reshape | solution.py:336
  57.9 1.4 copy.54.slot_column
  62.4 11.0 %shard_map.196 = (f32[2048,512]{1,0:T(8,128)}, f32[512,512]{1,0:T(8,128)}, f32[512,512]{1,0:T(8,128)}, f32[3,512,1024]{2,1,0:T(8,128)}, f32[512,1024]{1,0:T(8,128)}) custom-call(bf16[512,512]{1,0:T(8,128)(2,1)} %get-tuple-element.17.latent, s32[2048,1]{1,0:T(8,128)} %copy.53.recv_column, bf16[512,512]{1,0:T(8,128)(2,1)} %get-tuple-element.33.recv_w, ...), custom_call_target="tpu_custom_call" | custom-call | tf_op jit(solution)/shard_map/pallas_call | solution.py:214
  73.4 29.6 %all-to-all-done = bf16[32,64,512]{2,1,0:T(8,128)(2,1)S(1)} async-done(((bf16[32,64,512]{2,1,0:T(8,128)(2,1)}), bf16[32,64,512]{2,1,0:T(8,128)(2,1)S(1)}, u32[]{:S(2)}, u32[]{:S(2)}) %all-to-all-start) | async-done | bytes 2097184 | tf_op jit(solution)/shard_map/all_to_all | solution.py:325
  103.0 1.4 copy-done
  104.3 15.5 %shard_map.197 = (bf16[512,512]{1,0:T(8,128)(2,1)}, bf16[512,512]{1,0:T(8,128)(2,1)}, bf16[512,128]{1,0:T(8,128)(2,1)}, bf16[512,128]{1,0:T(8,128)(2,1)}) custom-call(bf16[2048,512]{1,0:T(8,128)(2,1)} %bitcast.96, s32[2048,1]{1,0:T(8,128)} %copy.54.slot_column, f32[2048,512]{1,0:T(8,128)} %get-tuple-element.19.recv_terms, s32[1,2048]{1,0:T(1,128)} %bitcast.102, ...), custom_call_target="tpu_custom_call" | custom-call | tf_op jit(solution)/shard_map/pallas_call | solution.py:214
  120.0 5.2 %collective-permute-start.3 = (bf16[512,128]{1,0:T(8,128)(2,1)}, bf16[512,128]{1,0:T(8,128)(2,1)S(1)}, u32[]{:S(2)}, u32[]{:S(2)}) collective-permute-start(bf16[512,128]{1,0:T(8,128)(2,1)} %get-tuple-element.23), channel_id=1, source_target_pairs={{1,0},{2,1},{3,2},{4,3},{5,4},{6,5},{7,6},{8,7},{9,8},{10,9},{11,1... | collective-permute-start | bytes 393224 | tf_op jit(solution)/shard_map/ppermute | solution.py:235
  126.6 7.1 %shard_map.198.terms = f32[3,512,1024]{2,1,0:T(8,128)} custom-call(bf16[512,512]{1,0:T(8,128)(2,1)} %get-tuple-element.24.send, s32[3,1,1024]{2,1,0:T(1,128)} %copy.56.index, f32[3,512,1024]{2,1,0:T(8,128)} %get-tuple-element.25.terms), custom_call_target="tpu_custom_call" | custom-call | tf_op jit(solution)/shard_map/pallas_call | solution.py:399
  134.4 11.5 %shard_map.199 = f32[227,1024]{1,0:T(8,128)} custom-call(bf16[512,128]{1,0:T(8,128)(2,1)} %copy-done.2, bf16[512,128]{1,0:T(8,128)(2,1)} %copy-done.3, s32[3,1,1024]{2,1,0:T(1,128)} %select_n.13.index, f32[3,512,1024]{2,1,0:T(8,128)} %shard_map.198.terms, bf16[512,512]{1,0:T(8,128)(2,1)} %get-tuple-element.36.edge_w, f32[512,1]{1,0:T(8,128)} %get-tuple-element.43.edge_gain, ...), custom_call_target="tpu_custom_call" | custom-call | tf_op jit(solution)/shard_map/pallas_call | solution.py:408
  (68 shorter events, 12.2 us)
Async XLA Ops:
  0.6 15.1 %copy-start.1 = (bf16[512,227]{0,1:T(8,128)(2,1)S(1)}, bf16[512,227]{0,1:T(8,128)(2,1)}, u32[]{:S(2)}) copy-start(bf16[512,227]{0,1:T(8,128)(2,1)} %param.20) | copy-start | bytes 697348
  1.7 31.8 %collective-permute-start = (bf16[227,256]{1,0:T(8,128)(2,1)S(1)}, bf16[227,256]{1,0:T(8,128)(2,1)S(1)}, u32[]{:S(2)}, u32[]{:S(2)}) collective-permute-start(bf16[227,256]{1,0:T(8,128)(2,1)S(1)} %get-tuple-element.42), channel_id=1, source_target_pairs={{0,1},{1,2},{2,3},{3,4},{4,5},{5,6},{6,7},{7,8},{8,9},{9,10},{10,1... | collective-permute-start | bytes 348680 | tf_op jit(solution)/shard_map/ppermute | solution.py:235
  4.7 28.8 %collective-permute-start.1 = (bf16[227,256]{1,0:T(8,128)(2,1)S(1)}, bf16[227,256]{1,0:T(8,128)(2,1)S(1)}, u32[]{:S(2)}, u32[]{:S(2)}) collective-permute-start(bf16[227,256]{1,0:T(8,128)(2,1)S(1)} %get-tuple-element.41), channel_id=1, source_target_pairs={{1,0},{2,1},{3,2},{4,3},{5,4},{6,5},{7,6},{8,7},{9,8},{10,9},{11,1... | collective-permute-start | bytes 348680 | tf_op jit(solution)/shard_map/ppermute | solution.py:235
  16.6 4.2 %copy-start.13 = (s32[1536]{0:T(1024)S(1)}, s32[1536]{0:T(1024)}, u32[]{:S(2)}) copy-start(s32[1536]{0:T(1024)} %param.33) | copy-start | bytes 18436
  20.8 3.3 %copy-start.10 = (bf16[4,1536]{1,0:T(4,128)(2,1)S(1)}, bf16[4,1536]{1,0:T(4,128)(2,1)}, u32[]{:S(2)}) copy-start(bf16[4,1536]{1,0:T(4,128)(2,1)} %param.29) | copy-start | bytes 36868
  20.8 4.1 %copy-start.14 = (s32[1536]{0:T(1024)S(1)}, s32[1536]{0:T(1024)}, u32[]{:S(2)}) copy-start(s32[1536]{0:T(1024)} %param.32) | copy-start | bytes 18436
  20.8 4.7 %copy-start.8 = (s32[32,64]{1,0:T(8,128)S(1)}, s32[32,64]{1,0:T(8,128)}, u32[]{:S(2)}) copy-start(s32[32,64]{1,0:T(8,128)} %param.36) | copy-start | bytes 24580
  33.5 0.6 copy-start.4
  33.5 0.7 copy-start.5
  34.2 19.6 %copy-start.15 = (s32[2048]{0:T(1024)S(1)}, s32[2048]{0:T(1024)}, u32[]{:S(2)}) copy-start(s32[2048]{0:T(1024)} %param.34) | copy-start | bytes 24580
  50.0 5.4 %copy-start.7 = (bf16[4,3072]{1,0:T(4,128)(2,1)S(1)}, bf16[4,3072]{1,0:T(4,128)(2,1)}, u32[]{:S(2)}) copy-start(bf16[4,3072]{1,0:T(4,128)(2,1)} %param.31) | copy-start | bytes 73732
  50.0 7.9 %copy-start.12 = (s32[2048]{0:T(1024)S(1)}, s32[2048]{0:T(1024)}, u32[]{:S(2)}) copy-start(s32[2048]{0:T(1024)} %param.35) | copy-start | bytes 24580
  50.0 9.3 %copy-start.11 = (s32[3072]{0:T(1024)S(1)}, s32[3072]{0:T(1024)}, u32[]{:S(2)}) copy-start(s32[3072]{0:T(1024)} %param.37) | copy-start | bytes 36868
  50.0 11.8 %copy-start.9 = (bf16[4,2048]{1,0:T(4,128)(2,1)S(1)}, bf16[4,2048]{1,0:T(4,128)(2,1)}, u32[]{:S(2)}) copy-start(bf16[4,2048]{1,0:T(4,128)(2,1)} %param.30) | copy-start | bytes 49156
  50.0 53.0 %all-to-all-start = ((bf16[32,64,512]{2,1,0:T(8,128)(2,1)}), bf16[32,64,512]{2,1,0:T(8,128)(2,1)S(1)}, u32[]{:S(2)}, u32[]{:S(2)}) async-start(bf16[32,64,512]{2,1,0:T(8,128)(2,1)} %bitcast.98), calls=%async_computation | async-start | bytes 4194304 | tf_op jit(solution)/shard_map/all_to_all | solution.py:325
  53.9 19.5 %copy-start.6 = (s32[2048]{0:T(1024)}, s32[2048]{0:T(1024)S(1)}, u32[]{:S(2)}) copy-start(s32[2048]{0:T(1024)S(1)} %broadcast_subtract_fusion.1) | copy-start | bytes 24580
  103.0 1.4 copy-start
  104.3 21.5 %copy-start.16 = (f32[227]{0:T(256)S(1)}, f32[227]{0:T(256)}, u32[]{:S(2)}) copy-start(f32[227]{0:T(256)} %param.28) | copy-start | bytes 2728
  119.8 13.9 %collective-permute-start.2 = (bf16[512,128]{1,0:T(8,128)(2,1)}, bf16[512,128]{1,0:T(8,128)(2,1)S(1)}, u32[]{:S(2)}, u32[]{:S(2)}) collective-permute-start(bf16[512,128]{1,0:T(8,128)(2,1)} %get-tuple-element.22), channel_id=1, source_target_pairs={{0,1},{1,2},{2,3},{3,4},{4,5},{5,6},{6,7},{7,8},{8,9},{9,10},{10,1... | collective-permute-start | bytes 393224 | tf_op jit(solution)/shard_map/ppermute | solution.py:235
  120.0 13.7 %collective-permute-start.3 = (bf16[512,128]{1,0:T(8,128)(2,1)}, bf16[512,128]{1,0:T(8,128)(2,1)S(1)}, u32[]{:S(2)}, u32[]{:S(2)}) collective-permute-start(bf16[512,128]{1,0:T(8,128)(2,1)} %get-tuple-element.23), channel_id=1, source_target_pairs={{1,0},{2,1},{3,2},{4,3},{5,4},{6,5},{7,6},{8,7},{9,8},{10,9},{11,1... | collective-permute-start | bytes 393224 | tf_op jit(solution)/shard_map/ppermute | solution.py:235
  133.7 0.7 copy-start.2
  133.7 0.7 copy-start.3

commit v2 on v0

v2 whole, which is shorter than its diff:
```python
import jax
import jax.numpy as jnp
from jax import lax
from jax.experimental import pallas as pl
from jax.experimental.pallas import tpu as pltpu
from jax.sharding import PartitionSpec as P

M_DEV = 512
BLOCK = 512
VMEM_LIMIT = 16 << 20

eps = 1e-05
bf16 = jnp.bfloat16
f32 = jnp.float32


def contract(left, right, left_dim, right_dim):
    return lax.dot_general(
        left, right, (((left_dim,), (right_dim,)), ((), ())), preferred_element_type=f32
    )


def nn(left, right):
    return contract(left, right, 1, 0)


def nt(left, right):
    return contract(left, right, 1, 1)


def tn(left, right):
    return contract(left, right, 0, 0)


def swish(values):
    half = values * 0.5
    return half * jnp.tanh(half) + half


def norm_columns(values, gain):
    count = 1.0 / values.shape[0]
    mean = jnp.sum(values, axis=0, keepdims=True) * count
    var = jnp.sum(values * values, axis=0, keepdims=True) * count - mean * mean
    return (values - mean) * lax.rsqrt(var + eps) * gain


def pick_rows(index_row, count):
    rows = lax.broadcasted_iota(jnp.int16, (count, index_row.shape[1]), 0)
    return jnp.where(rows == index_row.astype(jnp.int16), bf16(1), bf16(0))


def pick_columns(index_column, count):
    columns = lax.broadcasted_iota(jnp.int16, (index_column.shape[0], count), 1)
    return jnp.where(columns == index_column.astype(jnp.int16), bf16(1), bf16(0))


def blocks(total):
    return [pl.ds(start, BLOCK) for start in range(0, total, BLOCK)]


def embed_columns(x, embed_w, second_w, bias, gain):
    hidden = swish(tn(embed_w, x) + bias).astype(bf16)
    return norm_columns(nn(second_w, hidden), gain).astype(bf16)


class Fetch:
    def __init__(self, source, buffer, semaphore):
        self.copy = pltpu.make_async_copy(source, buffer, semaphore)
        self.copy.start()
        self.buffer = buffer
        self.arrived = False

    def __call__(self):
        if not self.arrived:
            self.copy.wait()
            self.arrived = True
        return self.buffer


def column(rows, i):
    return jnp.transpose(rows[...])[:, i : i + 1]


def index_row(index, part):
    return index[part].reshape(1, -1)


def index_column(index, part):
    row = index_row(index, part).astype(f32)
    return jnp.transpose(jnp.broadcast_to(row, (8, row.shape[1])))[:, :1].astype(jnp.int32)


def embed_kernel(x, embed_w, biases, second_w, gains, send_w, latent, send):
    bias = column(biases(), 0)
    for part in blocks(x().shape[1]):
        hidden = swish(tn(embed_w()[...], x()[:, part]) + bias).astype(bf16)
        cells = norm_columns(nn(second_w()[...], hidden), column(gains(), 0)).astype(bf16)
        latent[:, part] = cells
        send[:, part] = nn(send_w()[...], cells).astype(bf16)


def encode_kernel(
    grid_latent,
    own,
    low,
    high,
    embed_w,
    embed_second_w,
    send_w,
    biases,
    gains,
    geom,
    geom_w,
    send_index,
    recv_index,
    edge_w,
    rows,
    link_w,
    grid_latent_out,
    latent,
    outgoing,
    table,
    messages,
    sums,
    picks,
    staged,
    nodes_near,
    semaphores,
):
    copies = [pltpu.make_async_copy(grid_latent, grid_latent_out, semaphores.at[0])]
    copies[0].start()
    halo = jnp.concatenate([low[...], high[...]], axis=1)
    reach = halo.shape[1] // 2
    cells = own.shape[1]
    ext = cells + 2 * reach
    table[:, reach : reach + cells] = own[...]
    halo = embed_columns(
        halo, embed_w[...], embed_second_w[...], column(biases, 0), column(gains, 0)
    )
    halo = nn(send_w[...], halo).astype(bf16)
    table[:, :reach] = halo[:, :reach]
    table[:, reach + cells :] = halo[:, reach:]
    bias = column(biases, 1)
    gain = column(gains, 1)
    for part in blocks(geom.shape[1]):
        pre_act = nn(table[...], pick_rows(index_row(send_index, part), ext))
        pre_act = pre_act + tn(geom_w[...], geom[:, part]) + bias
        hidden = swish(pre_act).astype(bf16)
        messages[:, part] = norm_columns(nn(edge_w[...], hidden), gain).astype(bf16)
        sums[:, part] = pick_rows(index_row(recv_index, part), sums.shape[0])
    row_columns = jnp.transpose(rows[...].astype(f32))
    per_row, count = row_columns.shape
    lanes = lax.broadcasted_iota(jnp.int32, (per_row, latent.shape[0]), 1).astype(f32)
    for i in range(count):
        picked = jnp.where(lanes == row_columns[:, i : i + 1], 1.0, 0.0)
        picks[i * per_row : (i + 1) * per_row, :] = picked.astype(bf16)
    nodes = nt(sums[...], messages[...]).astype(bf16)
    nodes_near[...] = nodes
    copies.append(pltpu.make_async_copy(nodes_near, latent, semaphores.at[1]))
    copies[-1].start()
    link = nt(nodes, link_w[...]).astype(bf16)
    for part in blocks(outgoing.shape[0]):
        staged[part, :] = nn(picks[part, :], link).astype(bf16)
        copies.append(
            pltpu.make_async_copy(
                staged.at[part, :], outgoing.at[part, :], semaphores.at[len(copies)]
            )
        )
        copies[-1].start()
    for copy in copies:
        copy.wait()


def window_kernel(
    latent,
    mesh_geom,
    recv_w,
    biases,
    mesh_geom_w,
    recv_index,
    node_w,
    grid_latent,
    decode_w,
    out_w,
    cell_geom_w,
    cell_geom,
    recv_terms,
    node_terms,
    latent_columns,
    cell_terms,
    out_terms,
):
    nodes = latent()[...]
    recv_bias = biases()[2:3, :]
    for part in blocks(recv_terms.shape[0]):
        picked = pick_columns(index_column(recv_index(), part), nodes.shape[0])
        picked = nn(picked, nodes).astype(bf16)
        terms = nt(picked, recv_w()[...]) + tn(mesh_geom()[:, part], mesh_geom_w()[...])
        recv_terms[part, :] = terms + recv_bias
    node_terms[...] = nt(node_w()[...], nodes) + column(biases(), 3)
    latent_columns[...] = jnp.transpose(nodes.astype(f32)).astype(bf16)
    cell_bias = column(biases(), 4)
    out_bias = column(biases(), 5)
    for part in blocks(grid_latent().shape[1]):
        cells = grid_latent()[:, part]
        out_terms[:, part] = nn(out_w()[...], cells) + out_bias
        terms = nn(decode_w()[...], cells) + cell_bias
        for k in range(cell_terms.shape[0]):
            cell_terms[k, :, part] = terms + tn(cell_geom_w()[...], cell_geom()[k, :, part])


def mesh_kernel(slot_index, edge_w, gains, recv_index, *refs):
    *recv_terms, node_w, node_terms, node_second_w, latent_columns, send_w = refs[:-8]
    arrived, state, send, send_low, send_high, messages, staged, semaphore = refs[-8:]
    reach = send_low.shape[1]
    sums = []
    for part, terms in zip(blocks(messages.shape[1]), recv_terms):
        picks = pick_columns(index_column(slot_index(), part), arrived.shape[0])
        hidden = swish(nn(picks, arrived[...]) + terms()[...]).astype(bf16)
        normed = norm_columns(nt(edge_w()[...], hidden), column(gains(), 2))
        messages[:, part] = normed.astype(bf16)
        sums.append(pick_rows(index_row(recv_index(), part), state.shape[1]))
    nodes = nt(jnp.concatenate(sums, axis=1), messages[...]).astype(bf16)
    hidden = swish(nt(node_w()[...], nodes) + node_terms()[...]).astype(bf16)
    normed = norm_columns(nn(node_second_w()[...], hidden), column(gains(), 3))
    values = (latent_columns()[...].astype(f32) + normed).astype(bf16)
    staged[...] = values
    copy = pltpu.make_async_copy(staged, state, semaphore)
    copy.start()
    sent = nn(send_w()[...], values).astype(bf16)
    send[...] = sent
    send_low[...] = sent[:, :reach]
    send_high[...] = sent[:, sent.shape[1] - reach :]
    copy.wait()


def local_kernel(index, *refs):
    *terms, send, out = refs
    for k in range(out.shape[0]):
        for part in blocks(out.shape[2]):
            picks = pick_rows(index()[k, :, part], send.shape[1])
            out[k, :, part] = terms[k]()[:, part] + nn(send[...], picks)


def decode_kernel(
    low,
    high,
    index,
    terms,
    edge_w,
    gains,
    gathered_w,
    out_terms,
    out_w,
    out_bias,
    prediction,
    staged,
    semaphores,
):
    halo = jnp.concatenate([low[...], high[...]], axis=1)
    gain = column(gains, 4)
    copies = []
    for part in blocks(terms.shape[2]):
        total = None
        for k in range(terms.shape[0]):
            picks = pick_rows(index[k, :, part], halo.shape[1])
            hidden = swish(terms[k, :, part] + nn(halo, picks)).astype(bf16)
            message = norm_columns(nn(edge_w[...], hidden), gain).astype(bf16).astype(f32)
            total = message if total is None else total + message
        pre_act = out_terms[:, part] + nn(gathered_w[...], total.astype(bf16))
        hidden = swish(pre_act).astype(bf16)
        staged[:, part] = nn(out_w[...], hidden) + out_bias[...]
        copies.append(
            pltpu.make_async_copy(
                staged.at[:, part], prediction.at[:, part], semaphores.at[len(copies)]
            )
        )
        copies[-1].start()
    for copy in copies:
        copy.wait()


def part_shape(shape, index):
    lead = tuple(part.size for part in index if isinstance(part, pl.Slice))
    return lead + shape[len(index) :]


def fetching(
    kernel,
    outs,
    fetched=(),
    resident=(),
    carried=(),
    scratch=(),
    in_place=(),
    limit=VMEM_LIMIT,
):
    pairs = [item if isinstance(item, tuple) else (item, ()) for item in fetched]
    n_in, n_res, n_out = len(pairs), len(resident), len(outs)
    extra = []
    for item in carried:
        if isinstance(item, int):
            extra.append(item)
        else:
            pairs.append(item if isinstance(item, tuple) else (item, ()))
            extra.append(len(pairs) - 1)
    arrays = [array for array, _ in pairs]
    shapes = [(part_shape(array.shape, index), array.dtype) for array, index in pairs]
    local = [i for i in range(len(pairs)) if i not in extra]

    def run(*refs):
        sources, refs = refs[: len(pairs)], refs[len(pairs) :]
        near, refs = refs[:n_res], refs[n_res:]
        results, refs = refs[:n_out], refs[n_out:]
        passed, refs = refs[: len(extra)], refs[len(extra) :]
        buffers = dict(zip(extra, passed))
        buffers.update(zip(local, refs[: len(local)]))
        refs = refs[len(local) :]
        copies = []
        if pairs:
            for i, (source, (_, index)) in enumerate(zip(sources, pairs)):
                source = source.at[index] if index else source
                copies.append(Fetch(source, buffers[i], refs[0].at[i]))
            refs = refs[1:]
        kernel(*copies[:n_in], *near, *results, *refs)
        for copy in copies:
            copy()

    near = pl.BlockSpec(memory_space=pltpu.VMEM)
    far = pl.BlockSpec(memory_space=pltpu.HBM)
    return pl.pallas_call(
        run,
        out_shape=tuple(outs) + tuple(pltpu.VMEM(*shapes[i]) for i in extra),
        in_specs=[far] * len(pairs) + [near] * n_res,
        out_specs=tuple(far if i in in_place else near for i in range(n_out))
        + (near,) * len(extra),
        scratch_shapes=[pltpu.VMEM(*shapes[i]) for i in local]
        + ([pltpu.SemaphoreType.DMA((len(pairs),))] if pairs else [])
        + list(scratch),
        compiler_params=pltpu.CompilerParams(vmem_limit_bytes=limit),
    )(
        *[pltpu.with_memory_space_constraint(value, pltpu.HBM) for value in arrays],
        *[pltpu.with_memory_space_constraint(value, pltpu.VMEM) for value in resident],
    )


def exchange(low_end, high_end):
    axes = ("space", "chan")
    count = lax.axis_size("space") * lax.axis_size("chan")
    up = [(i, (i + 1) % count) for i in range(count)]
    down = [(target, source) for source, target in up]
    return lax.ppermute(high_end, axes, up), lax.ppermute(low_end, axes, down)


def body(
    grid_in,
    grid_embed_w,
    g2m_w,
    pair_w,
    second_w,
    first_b,
    norm_gain,
    geom_w,
    out_w,
    out_b,
    g2m_geom,
    mesh_geom,
    m2g_geom,
    g2m_send,
    g2m_recv,
    mesh_recv,
    mesh_slot,
    mesh_rows,
    m2g_send,
):
    width = grid_embed_w.shape[0]
    cells = grid_in.shape[1]
    position = lax.axis_index(("space", "chan"))
    reach = cells // 4
    low, high = exchange(grid_in[:, :reach], grid_in[:, cells - reach :])

    kept = pltpu.VMEM
    shape = pltpu.HBM
    embed_t = grid_embed_w.T
    geom_t = geom_w.transpose(0, 2, 1)
    (
        grid_latent,
        own_send,
        embed_near,
        embed_second_near,
        g2m_near,
        bias_near,
        gain_near,
        geom_near,
        geom_w_near,
        send_near,
        recv_near,
        edge_near,
        rows_near,
        link_near,
    ) = fetching(
        embed_kernel,
        (kept((width, cells), bf16), kept((width, cells), bf16)),
        [grid_in, embed_t, first_b, (second_w, (0,)), norm_gain, g2m_w],
        carried=[
            1,
            3,
            5,
            2,
            4,
            g2m_geom,
            (geom_t, (0,)),
            g2m_send - position * cells + reach,
            g2m_recv - position * M_DEV,
            (second_w, (1,)),
            mesh_rows,
            (pair_w, (0, 0)),
        ],
    )

    edges = g2m_geom.shape[1]
    slots = mesh_rows.size
    grid_latent, latent, outgoing = fetching(
        encode_kernel,
        (
            shape((width, cells), bf16),
            shape((M_DEV, width), bf16),
            shape((slots, width), bf16),
        ),
        resident=[
            grid_latent,
            own_send,
            low,
            high,
            embed_near,
            embed_second_near,
            g2m_near,
            bias_near,
            gain_near,
            geom_near,
            geom_w_near,
            send_near,
            recv_near,
            edge_near,
            rows_near,
            link_near,
        ],
        scratch=[
            pltpu.VMEM((width, cells + 2 * reach), bf16),
            pltpu.VMEM((width, edges), bf16),
            pltpu.VMEM((M_DEV, edges), bf16),
            pltpu.VMEM((slots, M_DEV), bf16),
            pltpu.VMEM((slots, width), bf16),
            pltpu.VMEM((M_DEV, width), bf16),
            pltpu.SemaphoreType.DMA((2 + slots // BLOCK,)),
        ],
        in_place=(0, 1, 2),
    )
    arrived = lax.all_to_all(
        outgoing.reshape(mesh_rows.shape + (width,)),
        ("space", "chan"),
        split_axis=0,
        concat_axis=0,
        tiled=True,
    ).reshape(-1, width)

    mesh_edges = mesh_geom.shape[1]
    mesh_reach = M_DEV // 4
    recv_local = mesh_recv - position * M_DEV
    per_cell = m2g_send.shape[0] // cells
    cell_geom = m2g_geom.reshape(-1, cells, per_cell).transpose(2, 0, 1)
    own_index = (m2g_send - position * M_DEV).reshape(cells, per_cell).T[:, None, :]
    halo_index = jnp.where(
        own_index < 0,
        own_index + mesh_reach,
        jnp.where(own_index >= M_DEV, own_index - M_DEV + mesh_reach, -1),
    )
    recv_terms, node_terms, latent_columns, cell_terms, out_terms = fetching(
        window_kernel,
        (
            shape((mesh_edges, width), f32),
            shape((width, M_DEV), f32),
            shape((width, M_DEV), bf16),
            shape((per_cell, width, cells), f32),
            shape((width, cells), f32),
        ),
        [
            latent,
            mesh_geom,
            (pair_w, (0, 1)),
            first_b,
            (geom_t, (1,)),
            recv_local,
            (pair_w, (1, 0)),
            grid_latent,
            (pair_w, (2, 1)),
            (pair_w, (3, 0)),
            (geom_t, (2,)),
            cell_geom,
        ],
        limit=40 << 20,
    )

    state, send, send_low, send_high = fetching(
        mesh_kernel,
        (
            shape((width, M_DEV), bf16),
            kept((width, M_DEV), bf16),
            kept((width, mesh_reach), bf16),
            kept((width, mesh_reach), bf16),
        ),
        [mesh_slot, (second_w, (2,)), norm_gain, recv_local]
        + [(recv_terms, (part,)) for part in blocks(mesh_edges)]
        + [
            (pair_w, (1, 1)),
            node_terms,
            (second_w, (3,)),
            latent_columns,
            (pair_w, (2, 0)),
        ],
        resident=[arrived],
        scratch=[
            pltpu.VMEM((width, mesh_edges), bf16),
            pltpu.VMEM((width, M_DEV), bf16),
            pltpu.SemaphoreType.DMA(()),
        ],
        in_place=(0,),
        limit=32 << 20,
    )
    low, high = exchange(send_low, send_high)
    (
        cell_terms,
        halo_near,
        decode_near,
        gain_near,
        gathered_near,
        out_terms,
        out_w_near,
        out_b_near,
    ) = fetching(
        local_kernel,
        (kept(cell_terms.shape, f32),),
        [own_index] + [(cell_terms, (k,)) for k in range(per_cell)],
        resident=[send],
        carried=[
            halo_index,
            (second_w, (4,)),
            norm_gain,
            (pair_w, (3, 1)),
            out_terms,
            out_w,
            out_b[:, None],
        ],
    )
    (prediction,) = fetching(
        decode_kernel,
        (shape((out_w.shape[0], cells), f32),),
        resident=[
            low,
            high,
            halo_near,
            cell_terms,
            decode_near,
            gain_near,
            gathered_near,
            out_terms,
            out_w_near,
            out_b_near,
        ],
        scratch=[
            pltpu.VMEM((out_w.shape[0], cells), f32),
            pltpu.SemaphoreType.DMA((cells // BLOCK,)),
        ],
        in_place=(0,),
    )
    return (prediction, state)


def solution(mesh):
    split = ("space", "chan")
    return jax.shard_map(
        body,
        mesh=mesh,
        in_specs=(
            P(None, split),
            P(),
            P(),
            P(),
            P(),
            P(),
            P(),
            P(),
            P(),
            P(),
            P(None, split),
            P(None, split),
            P(None, split),
            P(split),
            P(split),
            P(split),
            P(split),
            P(split, None),
            P(split),
        ),
        out_specs=(P(None, split), P(None, split)),
        check_vma=False,
    )
```

time: 194 us -> 110 us (0.57)
  local copies, waits for them, and re-layouts: 81.4 us -> 6.73 us
  matrix products: 49.1 us -> 0 us
  Pallas kernels: 0 us -> 48.7 us
  other arithmetic: 12.8 us -> 1.93 us
  waiting for transfers between devices: 33.6 us -> 36.5 us
    dot_general x12 -> x0, matrix products: 49.1 us -> none  [the longest x10 41.7 us: by_rows(): lax.dot_general(values, weight, (((1,), (1,)), ((), ())), preferred_eleme...]
    pallas_call x0 -> x6, Pallas kernels: none -> 48.7 us  [fetching(): pl.pallas_call(run, out_shape=tuple(outs) + tuple((pltpu.VMEM(*shapes[i])...]
    gather x5 -> x0, local copies, waits for them, and re-layouts: 45.3 us -> none  [the longest x1 13.2 us: body(): widened[mesh_sender].astype(jnp.float32) + expanded]
    all_to_all x1, waiting for transfers between devices: 16.9 us -> 32.9 us  [body(): lax.all_to_all(outgoing.reshape(mesh_rows.shape + (width,)), ('space', 'c...]
    ppermute x4, waiting for transfers between devices: 16.8 us -> 3.59 us  [exchange(): return (lax.ppermute(high_end, axes, up), lax.ppermute(low_end, axes, down))]
    reshape x3 -> x4, local copies, waits for them, and re-layouts: 15.2 us -> 3.7 us  [the longest x2 3.17 us: body(): cell_geom = m2g_geom.reshape(-1, cells, per_cell).transpose(2, 0, 1)]
    reduce_sum x1 -> x0, other arithmetic: 7.28 us -> none  [body(): message.astype(jnp.float32).reshape(grid_cells, 3, width).sum(axis=1)]
    slice x8 -> x1, local copies, waits for them, and re-layouts: 8.2 us -> 0.98 us  [body(): low, high = exchange(grid_in[:, :reach], grid_in[:, cells - reach:])]
  transfers between devices with their start and end apart: 5 -> 5, of which waited for: 5 -> 2; matrix products, arithmetic and copies ran while one was open for 18% -> 7% of each run, Pallas kernels for 0% -> 18%
where the time goes in v2:
time: 110 us
  Pallas kernels  48.7 us (44%)
  waiting for transfers between devices  36.5 us (33%)
  starting transfers between devices  14.8 us (13%)
  local copies, waits for them, and re-layouts  6.73 us (6%)
  other arithmetic  1.93 us (2%)
    pallas_call x6, Pallas kernels, fetching(): pl.pallas_call(run, out_shape=tuple(outs) + tuple((pltpu.VMEM(*shapes[i])...  48.7 us
    all_to_all x1, waiting for transfers between devices, body(): lax.all_to_all(outgoing.reshape(mesh_rows.shape + (width,)), ('space', 'c...  32.9 us
    ppermute x4, starting transfers between devices, exchange(): return (lax.ppermute(high_end, axes, up), lax.ppermute(low_end, axes, down))  11.9 us
    ppermute x4, waiting for transfers between devices, exchange(): return (lax.ppermute(high_end, axes, up), lax.ppermute(low_end, axes, down))  3.59 us
    reshape x2, local copies, waits for them, and re-layouts, body(): cell_geom = m2g_geom.reshape(-1, cells, per_cell).transpose(2, 0, 1)  3.17 us
    all_to_all x1, starting transfers between devices, body(): lax.all_to_all(outgoing.reshape(mesh_rows.shape + (width,)), ('space', 'c...  2.92 us
  transfers between devices with their start and end apart: 5, of which 2 were waited for; matrix products, arithmetic and copies ran while one was open for 7% of the time, Pallas kernels for 18%

profile of v2, /device:TPU:0, one launch (start us, length us, event | category | flops | bytes accessed | tf_op | source)
XLA Modules:
  0.0 109.6 jit_solution(5248048367471516389)
XLA Ops:
  0.6 1.0 fusion.2
  1.6 6.5 %collective-permute-start.1 = (bf16[227,256]{1,0:T(8,128)(2,1)S(1)}, bf16[227,256]{1,0:T(8,128)(2,1)S(1)}, u32[]{:S(2)}, u32[]{:S(2)}) collective-permute-start(bf16[227,256]{1,0:T(8,128)(2,1)S(1)} %get-tuple-element.70), channel_id=1, source_target_pairs={{1,0},{2,1},{3,2},{4,3},{5,4},{6,5},{7,6},{8,7},{9,8},{10,9},{11,1... | collective-permute-start | bytes 348680 | tf_op jit(solution)/shard_map/ppermute | solution.py:352
  8.1 1.3 %subtract_add_fusion = (s32[1536]{0:T(1024)}, s32[1536]{0:T(1024)}) fusion(s32[1536]{0:T(1024)} %param.32, s32[]{:T(128)S(6)} %mul.13, s32[1536]{0:T(1024)} %param.33, s32[]{:T(128)S(6)} %mul.12), kind=kLoop, calls=%fused_computation.6 | loop fusion | flops 4608 | bytes 24584 | tf_op jit(solution)/shard_map/add | solution.py:413
  9.4 4.2 %shard_map.194 = (bf16[512,1024]{1,0:T(8,128)(2,1)S(1)}, bf16[512,1024]{1,0:T(8,128)(2,1)S(1)}, bf16[227,512]{1,0:T(8,128)(2,1)S(1)}, bf16[512,512]{1,0:T(8,128)...) custom-call(bf16[227,1024]{1,0:T(8,128)(2,1)} %refs_0_.2, ...), custom_call_target="tpu_custom_call" | custom-call | tf_op jit(solution)/shard_map/pallas_call | solution.py:331
  13.6 3.6 %collective-permute-done.refs_2_ = bf16[227,256]{1,0:T(8,128)(2,1)S(1)} collective-permute-done((bf16[227,256]{1,0:T(8,128)(2,1)S(1)}, bf16[227,256]{1,0:T(8,128)(2,1)S(1)}, u32[]{:S(2)}, u32[]{:S(2)}) %collective-permute-start) | collective-permute-done | bytes 116256 | tf_op jit(solution)/shard_map/ppermute | solution.py:352
  17.2 8.7 %shard_map.195 = (bf16[512,1024]{1,0:T(8,128)(2,1)}, bf16[512,512]{1,0:T(8,128)(2,1)}, bf16[2048,512]{1,0:T(8,128)(2,1)}) custom-call(bf16[512,1024]{1,0:T(8,128)(2,1)S(1)} %get-tuple-element.36.refs_0_, bf16[512,1024]{1,0:T(8,128)(2,1)S(1)} %get-tuple-element.37.refs_1_, bf16[227,256]{1,0:T(8,128)(2,1)S(1)} %collective-permute-done.refs_2_, ...), custom_call_target="tpu_custom_call" | custom-call | tf_op jit(solution)/shard_map/pallas_call | solution.py:331
  25.9 0.0 copy-start.1
  25.9 0.0 copy-start
  25.9 2.9 %all-to-all-start = ((bf16[32,64,512]{2,1,0:T(8,128)(2,1)}), bf16[32,64,512]{2,1,0:T(8,128)(2,1)S(1)}, u32[]{:S(2)}, u32[]{:S(2)}) async-start(bf16[32,64,512]{2,1,0:T(8,128)(2,1)} %bitcast.24), calls=%async_computation | async-start | bytes 4194304 | tf_op jit(solution)/shard_map/all_to_all | solution.py:459
  28.9 0.8 copy.25.refs_10_
  29.7 0.3 reshape.26
  30.0 0.2 copy.23
  30.2 0.6 copy.24.refs_0_
  30.8 2.2 %reshape.23 = bf16[4,1024,3]{2,1,0:T(8,128)(2,1)S(1)} reshape(bf16[4,3072]{1,0:T(4,128)(2,1)S(1)} %copy-done) | data formatting | bytes 49152 | tf_op jit(solution)/shard_map/reshape | solution.py:471
  33.0 1.0 copy.22
  34.0 0.6 broadcast_subtract_fusion.2.refs_5_.refs_3_
  34.6 11.2 %shard_map.196 = (f32[2048,512]{1,0:T(8,128)}, f32[512,512]{1,0:T(8,128)}, bf16[512,512]{1,0:T(8,128)(2,1)}, f32[3,512,1024]{2,1,0:T(8,128)}, f32[512,1024]{1,0:T(8,128)}) custom-call(bf16[512,512]{1,0:T(8,128)(2,1)} %get-tuple-element.50.refs_0_, bf16[4,2048]{1,0:T(4,128)(2,1)} %refs_1_.2, bf16[4,2,512,512]{3,2,1,0:T(8,128)(2,1)} %refs_7_.1, ...), custom_call_target="tpu_custom_call" | custom-call | tf_op jit(solution)/shard_map/pallas_call | solution.py:331
  45.8 32.9 %all-to-all-done = bf16[32,64,512]{2,1,0:T(8,128)(2,1)S(1)} async-done(((bf16[32,64,512]{2,1,0:T(8,128)(2,1)}), bf16[32,64,512]{2,1,0:T(8,128)(2,1)S(1)}, u32[]{:S(2)}, u32[]{:S(2)}) %all-to-all-start) | async-done | bytes 2097184 | tf_op jit(solution)/shard_map/all_to_all | solution.py:459
  78.7 13.6 %shard_map.197 = (bf16[512,512]{1,0:T(8,128)(2,1)}, bf16[512,512]{1,0:T(8,128)(2,1)S(1)}, bf16[512,128]{1,0:T(8,128)(2,1)S(1)}, bf16[512,128]{1,0:T(8,128)(2,1)S(1)}) custom-call(s32[2048]{0:T(1024)} %refs_0_.3, bf16[5,512,512]{2,1,0:T(8,128)(2,1)} %refs_5_.3, f32[5,512]{1,0:T(8,128)} %refs_6_.5, s32[2048]{0:T(1024)} %broadcast_subtract_fusion.2.refs_5_.refs_3_, ...), custom_call_target="tpu_custom_call" | custom-call | tf_op jit(solution)/shard_map/pallas_call | solution.py:331
  92.3 0.2 collective-permute-start.2
  92.5 5.2 %collective-permute-start.3 = (bf16[512,128]{1,0:T(8,128)(2,1)S(1)}, bf16[512,128]{1,0:T(8,128)(2,1)S(1)}, u32[]{:S(2)}, u32[]{:S(2)}) collective-permute-start(bf16[512,128]{1,0:T(8,128)(2,1)S(1)} %get-tuple-element.57), channel_id=1, source_target_pairs={{1,0},{2,1},{3,2},{4,3},{5,4},{6,5},{7,6},{8,7},{9,8},{10,9},{11,1... | collective-permute-start | bytes 393224 | tf_op jit(solution)/shard_map/ppermute | solution.py:352
  97.7 0.6 select_n.13.refs_4_
  98.3 3.9 %shard_map.198 = (f32[3,512,1024]{2,1,0:T(8,128)S(1)}, s32[3,1,1024]{2,1,0:T(1,128)S(1)}, bf16[512,512]{1,0:T(8,128)(2,1)S(1)}, f32[5,512]{1,0:T(8,128)S(1)}, bf...) custom-call(s32[3,1,1024]{2,1,0:T(1,128)} %copy.24.refs_0_, ...), custom_call_target="tpu_custom_call" | custom-call | tf_op jit(solution)/shard_map/pallas_call | solution.py:331
  102.3 7.2 %shard_map.199 = f32[227,1024]{1,0:T(8,128)} custom-call(bf16[512,128]{1,0:T(8,128)(2,1)S(1)} %collective-permute-done.2.refs_0_, bf16[512,128]{1,0:T(8,128)(2,1)S(1)} %collective-permute-done.3.refs_1_, s32[3,1,1024]{2,1,0:T(1,128)S(1)} %get-tuple-element.61.refs_2_, f32[3,512,1024]{2,1,0:T(8,128)S(1)} %get-tuple-element.62.refs_3_, ...), custom_call_target="tpu_custom_call" | custom-call | tf_op jit(solution)/shard_map/pallas_call | solution.py:331
  (12 shorter events, 0.0 us)
Async XLA Ops:
  1.6 11.9 %collective-permute-start.1 = (bf16[227,256]{1,0:T(8,128)(2,1)S(1)}, bf16[227,256]{1,0:T(8,128)(2,1)S(1)}, u32[]{:S(2)}, u32[]{:S(2)}) collective-permute-start(bf16[227,256]{1,0:T(8,128)(2,1)S(1)} %get-tuple-element.70), channel_id=1, source_target_pairs={{1,0},{2,1},{3,2},{4,3},{5,4},{6,5},{7,6},{8,7},{9,8},{10,9},{11,1... | collective-permute-start | bytes 348680 | tf_op jit(solution)/shard_map/ppermute | solution.py:352
  8.1 9.1 %collective-permute-start = (bf16[227,256]{1,0:T(8,128)(2,1)S(1)}, bf16[227,256]{1,0:T(8,128)(2,1)S(1)}, u32[]{:S(2)}, u32[]{:S(2)}) collective-permute-start(bf16[227,256]{1,0:T(8,128)(2,1)S(1)} %get-tuple-element.71), channel_id=1, source_target_pairs={{0,1},{1,2},{2,3},{3,4},{4,5},{5,6},{6,7},{7,8},{8,9},{9,10},{10,1... | collective-permute-start | bytes 348680 | tf_op jit(solution)/shard_map/ppermute | solution.py:352
  25.9 3.0 %copy-start.3 = (f32[227]{0:T(256)S(1)}, f32[227]{0:T(256)}, u32[]{:S(2)}) copy-start(f32[227]{0:T(256)} %param.28) | copy-start | bytes 2728
  25.9 3.8 %copy-start.1 = (s32[3072]{0:T(1024)S(1)}, s32[3072]{0:T(1024)}, u32[]{:S(2)}) copy-start(s32[3072]{0:T(1024)} %param.37) | copy-start | bytes 36868
  25.9 4.9 %copy-start = (bf16[4,3072]{1,0:T(4,128)(2,1)S(1)}, bf16[4,3072]{1,0:T(4,128)(2,1)}, u32[]{:S(2)}) copy-start(bf16[4,3072]{1,0:T(4,128)(2,1)} %param.31) | copy-start | bytes 73732
  25.9 52.8 %all-to-all-start = ((bf16[32,64,512]{2,1,0:T(8,128)(2,1)}), bf16[32,64,512]{2,1,0:T(8,128)(2,1)S(1)}, u32[]{:S(2)}, u32[]{:S(2)}) async-start(bf16[32,64,512]{2,1,0:T(8,128)(2,1)} %bitcast.24), calls=%async_computation | async-start | bytes 4194304 | tf_op jit(solution)/shard_map/all_to_all | solution.py:459
  28.8 5.2 %copy-start.2 = (s32[2048]{0:T(1024)S(1)}, s32[2048]{0:T(1024)}, u32[]{:S(2)}) copy-start(s32[2048]{0:T(1024)} %param.34) | copy-start | bytes 24580
  92.3 9.9 %collective-permute-start.2 = (bf16[512,128]{1,0:T(8,128)(2,1)S(1)}, bf16[512,128]{1,0:T(8,128)(2,1)S(1)}, u32[]{:S(2)}, u32[]{:S(2)}) collective-permute-start(bf16[512,128]{1,0:T(8,128)(2,1)S(1)} %get-tuple-element.56), channel_id=1, source_target_pairs={{0,1},{1,2},{2,3},{3,4},{4,5},{5,6},{6,7},{7,8},{8,9},{9,10},{10,1... | collective-permute-start | bytes 393224 | tf_op jit(solution)/shard_map/ppermute | solution.py:352
  92.5 9.7 %collective-permute-start.3 = (bf16[512,128]{1,0:T(8,128)(2,1)S(1)}, bf16[512,128]{1,0:T(8,128)(2,1)S(1)}, u32[]{:S(2)}, u32[]{:S(2)}) collective-permute-start(bf16[512,128]{1,0:T(8,128)(2,1)S(1)} %get-tuple-element.57), channel_id=1, source_target_pairs={{1,0},{2,1},{3,2},{4,3},{5,4},{6,5},{7,6},{8,7},{9,8},{10,9},{11,1... | collective-permute-start | bytes 393224 | tf_op jit(solution)/shard_map/ppermute | solution.py:352

commit v3 on v2

--- a/solution.py
+++ b/solution.py
@@ -5,6 +5,7 @@
 from jax.experimental.pallas import tpu as pltpu
 from jax.sharding import PartitionSpec as P
 
+
 M_DEV = 512
 BLOCK = 512
 VMEM_LIMIT = 16 << 20
@@ -85,23 +86,63 @@
     return index[part].reshape(1, -1)
 
 
+def outside(index, count, reach):
+    beyond = jnp.where(index >= count, index - count + reach, -1)
+    return jnp.where(index < 0, index + reach, beyond)
+
+
 def index_column(index, part):
     row = index_row(index, part).astype(f32)
     return jnp.transpose(jnp.broadcast_to(row, (8, row.shape[1])))[:, :1].astype(jnp.int32)
 
 
-def embed_kernel(x, embed_w, biases, second_w, gains, send_w, latent, send):
+def place():
+    return lax.axis_index("space") * lax.axis_size("chan") + lax.axis_index("chan")
+
+
+def embed_kernel(
+    x,
+    embed_w,
+    biases,
+    second_w,
+    gains,
+    send_w,
+    send_index,
+    geom,
+    geom_w,
+    recv_index,
+    rows,
+    latent,
+    own_terms,
+    sums,
+    picks,
+    table,
+):
     bias = column(biases(), 0)
-    for part in blocks(x().shape[1]):
+    cells = x().shape[1]
+    nodes = sums.shape[0]
+    for part in blocks(cells):
         hidden = swish(tn(embed_w()[...], x()[:, part]) + bias).astype(bf16)
-        cells = norm_columns(nn(second_w()[...], hidden), column(gains(), 0)).astype(bf16)
-        latent[:, part] = cells
-        send[:, part] = nn(send_w()[...], cells).astype(bf16)
+        values = norm_columns(nn(second_w()[...], hidden), column(gains(), 0)).astype(bf16)
+        latent[:, part] = values
+        table[:, part] = nn(send_w()[...], values).astype(bf16)
+    bias = column(biases(), 1)
+    for part in blocks(geom().shape[1]):
+        own = index_row(send_index(), part) - place() * cells
+        terms = nn(table[...], pick_rows(own, cells))
+        own_terms[:, part] = terms + tn(geom_w()[...], geom()[:, part]) + bias
+        sums[:, part] = pick_rows(index_row(recv_index(), part) - place() * nodes, nodes)
+    row_columns = jnp.transpose(rows()[...].astype(f32)).astype(jnp.int32)
+    per_row, count = row_columns.shape
+    for i in range(count):
+        picks[i * per_row : (i + 1) * per_row, :] = pick_columns(row_columns[:, i : i + 1], nodes)
 
 
 def encode_kernel(
     grid_latent,
-    own,
+    own_terms,
+    sums,
+    picks,
     low,
     high,
     embed_w,
@@ -109,20 +150,13 @@
     send_w,
     biases,
     gains,
-    geom,
-    geom_w,
     send_index,
-    recv_index,
     edge_w,
-    rows,
     link_w,
     grid_latent_out,
     latent,
     outgoing,
-    table,
     messages,
-    sums,
-    picks,
     staged,
     nodes_near,
     semaphores,
@@ -131,29 +165,17 @@
     copies[0].start()
     halo = jnp.concatenate([low[...], high[...]], axis=1)
     reach = halo.shape[1] // 2
-    cells = own.shape[1]
-    ext = cells + 2 * reach
-    table[:, reach : reach + cells] = own[...]
+    cells = grid_latent.shape[1]
     halo = embed_columns(
         halo, embed_w[...], embed_second_w[...], column(biases, 0), column(gains, 0)
     )
     halo = nn(send_w[...], halo).astype(bf16)
-    table[:, :reach] = halo[:, :reach]
-    table[:, reach + cells :] = halo[:, reach:]
-    bias = column(biases, 1)
     gain = column(gains, 1)
-    for part in blocks(geom.shape[1]):
-        pre_act = nn(table[...], pick_rows(index_row(send_index, part), ext))
-        pre_act = pre_act + tn(geom_w[...], geom[:, part]) + bias
+    for part in blocks(own_terms.shape[1]):
+        index = outside(index_row(send_index, part) - place() * cells, cells, reach)
+        pre_act = own_terms[:, part] + nn(halo, pick_rows(index, 2 * reach))
         hidden = swish(pre_act).astype(bf16)
         messages[:, part] = norm_columns(nn(edge_w[...], hidden), gain).astype(bf16)
-        sums[:, part] = pick_rows(index_row(recv_index, part), sums.shape[0])
-    row_columns = jnp.transpose(rows[...].astype(f32))
-    per_row, count = row_columns.shape
-    lanes = lax.broadcasted_iota(jnp.int32, (per_row, latent.shape[0]), 1).astype(f32)
-    for i in range(count):
-        picked = jnp.where(lanes == row_columns[:, i : i + 1], 1.0, 0.0)
-        picks[i * per_row : (i + 1) * per_row, :] = picked.astype(bf16)
     nodes = nt(sums[...], messages[...]).astype(bf16)
     nodes_near[...] = nodes
     copies.append(pltpu.make_async_copy(nodes_near, latent, semaphores.at[1]))
@@ -193,7 +215,8 @@
     nodes = latent()[...]
     recv_bias = biases()[2:3, :]
     for part in blocks(recv_terms.shape[0]):
-        picked = pick_columns(index_column(recv_index(), part), nodes.shape[0])
+        picked = index_column(recv_index(), part) - place() * nodes.shape[0]
+        picked = pick_columns(picked, nodes.shape[0])
         picked = nn(picked, nodes).astype(bf16)
         terms = nt(picked, recv_w()[...]) + tn(mesh_geom()[:, part], mesh_geom_w()[...])
         recv_terms[part, :] = terms + recv_bias
@@ -209,20 +232,30 @@
             cell_terms[k, :, part] = terms + tn(cell_geom_w()[...], cell_geom()[k, :, part])
 
 
-def mesh_kernel(slot_index, edge_w, gains, recv_index, *refs):
-    *recv_terms, node_w, node_terms, node_second_w, latent_columns, send_w = refs[:-8]
-    arrived, state, send, send_low, send_high, messages, staged, semaphore = refs[-8:]
+def mesh_kernel(edge_w, *refs):
+    *recv_terms, node_w, node_terms, node_second_w, latent_columns, send_w = refs[:-12]
+    slot_index, recv_index, gains = refs[-12:-9]
+    arrived, state, send, send_low, send_high = refs[-9:-4]
+    messages, gathered, staged, semaphore = refs[-4:]
     reach = send_low.shape[1]
+    count = state.shape[1]
+    parts = blocks(messages.shape[1])
+    gain = column(gains, 2)
+    ahead = 2
     sums = []
-    for part, terms in zip(blocks(messages.shape[1]), recv_terms):
-        picks = pick_columns(index_column(slot_index(), part), arrived.shape[0])
-        hidden = swish(nn(picks, arrived[...]) + terms()[...]).astype(bf16)
-        normed = norm_columns(nt(edge_w()[...], hidden), column(gains(), 2))
-        messages[:, part] = normed.astype(bf16)
-        sums.append(pick_rows(index_row(recv_index(), part), state.shape[1]))
+    for i in range(len(parts) + ahead):
+        if i < len(parts):
+            picks = pick_columns(index_column(slot_index, parts[i]), arrived.shape[0])
+            gathered[parts[i], :] = nn(picks, arrived[...])
+        if i >= ahead:
+            part = parts[i - ahead]
+            hidden = swish(gathered[part, :] + recv_terms[i - ahead]()[...]).astype(bf16)
+            messages[:, part] = norm_columns(nt(edge_w()[...], hidden), gain).astype(bf16)
+            index = index_row(recv_index, part) - place() * count
+            sums.append(pick_rows(index, count))
     nodes = nt(jnp.concatenate(sums, axis=1), messages[...]).astype(bf16)
     hidden = swish(nt(node_w()[...], nodes) + node_terms()[...]).astype(bf16)
-    normed = norm_columns(nn(node_second_w()[...], hidden), column(gains(), 3))
+    normed = norm_columns(nn(node_second_w()[...], hidden), column(gains, 3))
     values = (latent_columns()[...].astype(f32) + normed).astype(bf16)
     staged[...] = values
     copy = pltpu.make_async_copy(staged, state, semaphore)
@@ -238,7 +271,8 @@
     *terms, send, out = refs
     for k in range(out.shape[0]):
         for part in blocks(out.shape[2]):
-            picks = pick_rows(index()[k, :, part], send.shape[1])
+            picks = index()[k, :, part] - place() * send.shape[1]
+            picks = pick_rows(picks, send.shape[1])
             out[k, :, part] = terms[k]()[:, part] + nn(send[...], picks)
 
 
@@ -259,17 +293,21 @@
 ):
     halo = jnp.concatenate([low[...], high[...]], axis=1)
     gain = column(gains, 4)
+    offset = out_bias[...].reshape(1, -1)
+    offset = jnp.transpose(jnp.broadcast_to(offset, (8, offset.shape[1])))[:, :1]
     copies = []
     for part in blocks(terms.shape[2]):
         total = None
         for k in range(terms.shape[0]):
-            picks = pick_rows(index[k, :, part], halo.shape[1])
+            count = 2 * halo.shape[1]
+            picks = outside(index[k, :, part] - place() * count, count, halo.shape[1] // 2)
+            picks = pick_rows(picks, halo.shape[1])
             hidden = swish(terms[k, :, part] + nn(halo, picks)).astype(bf16)
             message = norm_columns(nn(edge_w[...], hidden), gain).astype(bf16).astype(f32)
             total = message if total is None else total + message
         pre_act = out_terms[:, part] + nn(gathered_w[...], total.astype(bf16))
         hidden = swish(pre_act).astype(bf16)
-        staged[:, part] = nn(out_w[...], hidden) + out_bias[...]
+        staged[:, part] = nn(out_w[...], hidden) + offset
         copies.append(
             pltpu.make_async_copy(
                 staged.at[:, part], prediction.at[:, part], semaphores.at[len(copies)]
@@ -349,7 +387,9 @@
     count = lax.axis_size("space") * lax.axis_size("chan")
     up = [(i, (i + 1) % count) for i in range(count)]
     down = [(target, source) for source, target in up]
-    return lax.ppermute(high_end, axes, up), lax.ppermute(low_end, axes, down)
+    low = lax.ppermute(high_end, axes, up)
+    high = lax.ppermute(low_end, axes, down)
+    return low, high
 
 
 def body(
@@ -375,7 +415,6 @@
 ):
     width = grid_embed_w.shape[0]
     cells = grid_in.shape[1]
-    position = lax.axis_index(("space", "chan"))
     reach = cells // 4
     low, high = exchange(grid_in[:, :reach], grid_in[:, cells - reach :])
 
@@ -383,43 +422,46 @@
     shape = pltpu.HBM
     embed_t = grid_embed_w.T
     geom_t = geom_w.transpose(0, 2, 1)
+    edges = g2m_geom.shape[1]
+    slots = mesh_rows.size
     (
         grid_latent,
-        own_send,
+        own_terms,
+        sums,
+        picks,
         embed_near,
         embed_second_near,
         g2m_near,
         bias_near,
         gain_near,
-        geom_near,
-        geom_w_near,
         send_near,
-        recv_near,
         edge_near,
-        rows_near,
         link_near,
     ) = fetching(
         embed_kernel,
-        (kept((width, cells), bf16), kept((width, cells), bf16)),
-        [grid_in, embed_t, first_b, (second_w, (0,)), norm_gain, g2m_w],
-        carried=[
-            1,
-            3,
-            5,
-            2,
-            4,
+        (
+            kept((width, cells), bf16),
+            kept((width, edges), f32),
+            kept((M_DEV, edges), bf16),
+            kept((slots, M_DEV), bf16),
+        ),
+        [
+            grid_in,
+            embed_t,
+            first_b,
+            (second_w, (0,)),
+            norm_gain,
+            g2m_w,
+            g2m_send,
             g2m_geom,
             (geom_t, (0,)),
-            g2m_send - position * cells + reach,
-            g2m_recv - position * M_DEV,
-            (second_w, (1,)),
+            g2m_recv,
             mesh_rows,
-            (pair_w, (0, 0)),
-        ],
-    )
-
-    edges = g2m_geom.shape[1]
-    slots = mesh_rows.size
+        ],
+        carried=[1, 3, 5, 2, 4, 6, (second_w, (1,)), (pair_w, (0, 0))],
+        scratch=[pltpu.VMEM((width, cells), bf16)],
+    )
+
     grid_latent, latent, outgoing = fetching(
         encode_kernel,
         (
@@ -429,7 +471,9 @@
         ),
         resident=[
             grid_latent,
-            own_send,
+            own_terms,
+            sums,
+            picks,
             low,
             high,
             embed_near,
@@ -437,19 +481,12 @@
             g2m_near,
             bias_near,
             gain_near,
-            geom_near,
-            geom_w_near,
             send_near,
-            recv_near,
             edge_near,
-            rows_near,
             link_near,
         ],
         scratch=[
-            pltpu.VMEM((width, cells + 2 * reach), bf16),
             pltpu.VMEM((width, edges), bf16),
-            pltpu.VMEM((M_DEV, edges), bf16),
-            pltpu.VMEM((slots, M_DEV), bf16),
             pltpu.VMEM((slots, width), bf16),
             pltpu.VMEM((M_DEV, width), bf16),
             pltpu.SemaphoreType.DMA((2 + slots // BLOCK,)),
@@ -466,15 +503,10 @@
 
     mesh_edges = mesh_geom.shape[1]
     mesh_reach = M_DEV // 4
-    recv_local = mesh_recv - position * M_DEV
     per_cell = m2g_send.shape[0] // cells
     cell_geom = m2g_geom.reshape(-1, cells, per_cell).transpose(2, 0, 1)
-    own_index = (m2g_send - position * M_DEV).reshape(cells, per_cell).T[:, None, :]
-    halo_index = jnp.where(
-        own_index < 0,
-        own_index + mesh_reach,
-        jnp.where(own_index >= M_DEV, own_index - M_DEV + mesh_reach, -1),
-    )
+    cell_send = m2g_send.reshape(cells, per_cell).T[:, None, :]
+    latent, cell_send = lax.optimization_barrier((latent, cell_send))
     recv_terms, node_terms, latent_columns, cell_terms, out_terms = fetching(
         window_kernel,
         (
@@ -490,7 +522,7 @@
             (pair_w, (0, 1)),
             first_b,
             (geom_t, (1,)),
-            recv_local,
+            mesh_recv,
             (pair_w, (1, 0)),
             grid_latent,
             (pair_w, (2, 1)),
@@ -509,7 +541,7 @@
             kept((width, mesh_reach), bf16),
             kept((width, mesh_reach), bf16),
         ),
-        [mesh_slot, (second_w, (2,)), norm_gain, recv_local]
+        [(second_w, (2,))]
         + [(recv_terms, (part,)) for part in blocks(mesh_edges)]
         + [
             (pair_w, (1, 1)),
@@ -518,9 +550,10 @@
             latent_columns,
             (pair_w, (2, 0)),
         ],
-        resident=[arrived],
+        resident=[mesh_slot, mesh_recv, norm_gain, arrived],
         scratch=[
             pltpu.VMEM((width, mesh_edges), bf16),
+            pltpu.VMEM((mesh_edges, width), f32),
             pltpu.VMEM((width, M_DEV), bf16),
             pltpu.SemaphoreType.DMA(()),
         ],
@@ -530,7 +563,7 @@
     low, high = exchange(send_low, send_high)
     (
         cell_terms,
-        halo_near,
+        send_near,
         decode_near,
         gain_near,
         gathered_near,
@@ -540,16 +573,16 @@
     ) = fetching(
         local_kernel,
         (kept(cell_terms.shape, f32),),
-        [own_index] + [(cell_terms, (k,)) for k in range(per_cell)],
+        [cell_send] + [(cell_terms, (k,)) for k in range(per_cell)],
         resident=[send],
         carried=[
-            halo_index,
+            0,
             (second_w, (4,)),
             norm_gain,
             (pair_w, (3, 1)),
             out_terms,
             out_w,
-            out_b[:, None],
+            out_b,
         ],
     )
     (prediction,) = fetching(
@@ -558,7 +591,7 @@
         resident=[
             low,
             high,
-            halo_near,
+            send_near,
             cell_terms,
             decode_near,
             gain_near,

time: 110 us -> 107 us (0.973)
  other arithmetic: 1.93 us -> 0 us
  local copies, waits for them, and re-layouts: 6.73 us -> 5.33 us
    ppermute x4, waiting for transfers between devices: 3.59 us -> 1.98 us  [the longest x2 1.97 us: exchange(): low = lax.ppermute(high_end, axes, up)]
    add x1 -> x0, other arithmetic: 1.32 us -> none  [body(): g2m_send - position * cells + reach]
    all_to_all x1, waiting for transfers between devices: 32.9 us -> 34 us  [body(): lax.all_to_all(outgoing.reshape(mesh_rows.shape + (width,)), ('space', 'c...]
  transfers between devices with their start and end apart: 5 -> 5, of which waited for: 2 -> 2; matrix products, arithmetic and copies ran while one was open for 7% -> 4% of each run, Pallas kernels for 18% -> 21%
where the time goes in v3:
time: 107 us; the launch traced here: 106 us
  Pallas kernels  48.2 us (45%)
  waiting for transfers between devices  36 us (34%)
  starting transfers between devices  15.8 us (15%)
  local copies, waits for them, and re-layouts  5.33 us (5%)
    pallas_call x6, Pallas kernels, fetching(): pl.pallas_call(run, out_shape=tuple(outs) + tuple((pltpu.VMEM(*shapes[i])...  48.2 us
    all_to_all x1, waiting for transfers between devices, body(): lax.all_to_all(outgoing.reshape(mesh_rows.shape + (width,)), ('space', 'c...  34 us
    ppermute x2, starting transfers between devices, exchange(): high = lax.ppermute(low_end, axes, down)  11.6 us
    all_to_all x1, starting transfers between devices, body(): lax.all_to_all(outgoing.reshape(mesh_rows.shape + (width,)), ('space', 'c...  3.94 us
    reshape x2, local copies, waits for them, and re-layouts, body(): cell_geom = m2g_geom.reshape(-1, cells, per_cell).transpose(2, 0, 1)  3.18 us
  transfers between devices with their start and end apart: 5, of which 2 were waited for; matrix products, arithmetic and copies ran while one was open for 4% of the time, Pallas kernels for 21%

profile of v3, /device:TPU:0, one launch (start us, length us, event | category | flops | bytes accessed | tf_op | source)
XLA Modules:
  0.0 106.3 jit_solution(2325046173703846598)
XLA Ops:
  0.6 1.0 fusion
  1.6 6.5 %collective-permute-start.1 = (bf16[227,256]{1,0:T(8,128)(2,1)S(1)}, bf16[227,256]{1,0:T(8,128)(2,1)S(1)}, u32[]{:S(2)}, u32[]{:S(2)}) collective-permute-start(bf16[227,256]{1,0:T(8,128)(2,1)S(1)} %get-tuple-element.70), channel_id=1, source_target_pairs={{1,0},{2,1},{3,2},{4,3},{5,4},{6,5},{7,6},{8,7},{9,8},{10,9},{11,1... | collective-permute-start | bytes 348680 | tf_op jit(solution)/shard_map/ppermute | solution.py:391
  8.1 0.0 collective-permute-start
  8.1 7.1 %shard_map.194 = (bf16[512,1024]{1,0:T(8,128)(2,1)S(1)}, f32[512,1536]{1,0:T(8,128)S(1)}, bf16[512,1536]{1,0:T(8,128)(2,1)S(1)}, bf16[2048,512]{1,0:T(8,128)(2,1...) custom-call(bf16[227,1024]{1,0:T(8,128)(2,1)} %refs_0_.2, ...), custom_call_target="tpu_custom_call" | custom-call | tf_op jit(solution)/shard_map/pallas_call | solution.py:369
  15.2 0.0 collective-permute-done.1.refs_5_
  15.2 2.0 %collective-permute-done.refs_4_ = bf16[227,256]{1,0:T(8,128)(2,1)S(1)} collective-permute-done((bf16[227,256]{1,0:T(8,128)(2,1)S(1)}, bf16[227,256]{1,0:T(8,128)(2,1)S(1)}, u32[]{:S(2)}, u32[]{:S(2)}) %collective-permute-start) | collective-permute-done | bytes 116256 | tf_op jit(solution)/shard_map/ppermute | solution.py:390
  17.2 6.9 %shard_map.195 = (bf16[512,1024]{1,0:T(8,128)(2,1)}, bf16[512,512]{1,0:T(8,128)(2,1)}, bf16[2048,512]{1,0:T(8,128)(2,1)}) custom-call(bf16[512,1024]{1,0:T(8,128)(2,1)S(1)} %get-tuple-element.36.refs_0_, f32[512,1536]{1,0:T(8,128)S(1)} %get-tuple-element.37.refs_1_, bf16[512,1536]{1,0:T(8,128)(2,1)S(1)} %get-tuple-element.38.refs_2_, ...), custom_call_target="tpu_custom_call" | custom-call | tf_op jit(solution)/shard_map/pallas_call | solution.py:369
  24.1 0.0 copy-start.4
  24.1 0.0 copy-start.3
  24.1 3.9 %all-to-all-start = ((bf16[32,64,512]{2,1,0:T(8,128)(2,1)}), bf16[32,64,512]{2,1,0:T(8,128)(2,1)S(1)}, u32[]{:S(2)}, u32[]{:S(2)}) async-start(bf16[32,64,512]{2,1,0:T(8,128)(2,1)} %bitcast.7), calls=%async_computation | async-start | bytes 4194304 | tf_op jit(solution)/shard_map/all_to_all | solution.py:496
  28.0 0.3 reshape.16
  28.4 0.2 copy.21
  28.6 0.6 broadcast_in_dim.3.refs_0_
  29.2 2.2 %reshape.17 = bf16[4,1024,3]{2,1,0:T(8,128)(2,1)S(1)} reshape(bf16[4,3072]{1,0:T(4,128)(2,1)S(1)} %copy-done.3) | data formatting | bytes 49152 | tf_op jit(solution)/shard_map/reshape | solution.py:507
  31.4 1.0 copy.22
  32.4 11.5 %shard_map.196 = (f32[2048,512]{1,0:T(8,128)}, f32[512,512]{1,0:T(8,128)}, bf16[512,512]{1,0:T(8,128)(2,1)}, f32[3,512,1024]{2,1,0:T(8,128)}, f32[512,1024]{1,0:T(8,128)}) custom-call(bf16[512,512]{1,0:T(8,128)(2,1)} %get-tuple-element.49.refs_0_, bf16[4,2048]{1,0:T(4,128)(2,1)} %refs_1_.1, bf16[4,2,512,512]{3,2,1,0:T(8,128)(2,1)} %refs_6_.5, ...), custom_call_target="tpu_custom_call" | custom-call | tf_op jit(solution)/shard_map/pallas_call | solution.py:369
  43.8 34.0 %all-to-all-done = bf16[32,64,512]{2,1,0:T(8,128)(2,1)S(1)} async-done(((bf16[32,64,512]{2,1,0:T(8,128)(2,1)}), bf16[32,64,512]{2,1,0:T(8,128)(2,1)S(1)}, u32[]{:S(2)}, u32[]{:S(2)}) %all-to-all-start) | async-done | bytes 2097184 | tf_op jit(solution)/shard_map/all_to_all | solution.py:496
  77.9 11.6 %shard_map.197 = (bf16[512,512]{1,0:T(8,128)(2,1)}, bf16[512,512]{1,0:T(8,128)(2,1)S(1)}, bf16[512,128]{1,0:T(8,128)(2,1)S(1)}, bf16[512,128]{1,0:T(8,128)(2,1)S(1)}) custom-call(bf16[5,512,512]{2,1,0:T(8,128)(2,1)} %refs_4_.3, f32[2048,512]{1,0:T(8,128)} %get-tuple-element.51.refs_1_.refs_2_.refs_3_.refs_4_, ...), custom_call_target="tpu_custom_call" | custom-call | tf_op jit(solution)/shard_map/pallas_call | solution.py:369
  89.6 0.2 collective-permute-start.2
  89.8 5.2 %collective-permute-start.3 = (bf16[512,128]{1,0:T(8,128)(2,1)S(1)}, bf16[512,128]{1,0:T(8,128)(2,1)S(1)}, u32[]{:S(2)}, u32[]{:S(2)}) collective-permute-start(bf16[512,128]{1,0:T(8,128)(2,1)S(1)} %get-tuple-element.56), channel_id=1, source_target_pairs={{1,0},{2,1},{3,2},{4,3},{5,4},{6,5},{7,6},{8,7},{9,8},{10,9},{11,1... | collective-permute-start | bytes 393224 | tf_op jit(solution)/shard_map/ppermute | solution.py:391
  95.0 3.9 %shard_map.198 = (f32[3,512,1024]{2,1,0:T(8,128)S(1)}, s32[3,1,1024]{2,1,0:T(1,128)S(1)}, bf16[512,512]{1,0:T(8,128)(2,1)S(1)}, f32[5,512]{1,0:T(8,128)S(1)}, bf...) custom-call(s32[3,1,1024]{2,1,0:T(1,128)} %broadcast_in_dim.3.refs_0_, ...), custom_call_target="tpu_custom_call" | custom-call | tf_op jit(solution)/shard_map/pallas_call | solution.py:369
  98.9 0.0 collective-permute-done.2.refs_0_
  98.9 0.0 collective-permute-done.3.refs_1_
  98.9 7.2 %shard_map.199 = f32[227,1024]{1,0:T(8,128)} custom-call(bf16[512,128]{1,0:T(8,128)(2,1)S(1)} %collective-permute-done.2.refs_0_, bf16[512,128]{1,0:T(8,128)(2,1)S(1)} %collective-permute-done.3.refs_1_, s32[3,1,1024]{2,1,0:T(1,128)S(1)} %get-tuple-element.61.refs_2_, f32[3,512,1024]{2,1,0:T(8,128)S(1)} %get-tuple-element.62.refs_3_, ...), custom_call_target="tpu_custom_call" | custom-call | tf_op jit(solution)/shard_map/pallas_call | solution.py:369
  (8 shorter events, 0.0 us)
Async XLA Ops:
  1.6 13.6 %collective-permute-start.1 = (bf16[227,256]{1,0:T(8,128)(2,1)S(1)}, bf16[227,256]{1,0:T(8,128)(2,1)S(1)}, u32[]{:S(2)}, u32[]{:S(2)}) collective-permute-start(bf16[227,256]{1,0:T(8,128)(2,1)S(1)} %get-tuple-element.70), channel_id=1, source_target_pairs={{1,0},{2,1},{3,2},{4,3},{5,4},{6,5},{7,6},{8,7},{9,8},{10,9},{11,1... | collective-permute-start | bytes 348680 | tf_op jit(solution)/shard_map/ppermute | solution.py:391
  8.1 9.1 %collective-permute-start = (bf16[227,256]{1,0:T(8,128)(2,1)S(1)}, bf16[227,256]{1,0:T(8,128)(2,1)S(1)}, u32[]{:S(2)}, u32[]{:S(2)}) collective-permute-start(bf16[227,256]{1,0:T(8,128)(2,1)S(1)} %get-tuple-element.71), channel_id=1, source_target_pairs={{0,1},{1,2},{2,3},{3,4},{4,5},{5,6},{6,7},{7,8},{8,9},{9,10},{10,1... | collective-permute-start | bytes 348680 | tf_op jit(solution)/shard_map/ppermute | solution.py:390
  24.1 4.0 %copy-start.4 = (s32[3072]{0:T(1024)S(1)}, s32[3072]{0:T(1024)}, u32[]{:S(2)}) copy-start(s32[3072]{0:T(1024)} %param.37) | copy-start | bytes 36868
  24.1 5.1 %copy-start.3 = (bf16[4,3072]{1,0:T(4,128)(2,1)S(1)}, bf16[4,3072]{1,0:T(4,128)(2,1)}, u32[]{:S(2)}) copy-start(bf16[4,3072]{1,0:T(4,128)(2,1)} %param.31) | copy-start | bytes 73732
  24.1 53.8 %all-to-all-start = ((bf16[32,64,512]{2,1,0:T(8,128)(2,1)}), bf16[32,64,512]{2,1,0:T(8,128)(2,1)S(1)}, u32[]{:S(2)}, u32[]{:S(2)}) async-start(bf16[32,64,512]{2,1,0:T(8,128)(2,1)} %bitcast.7), calls=%async_computation | async-start | bytes 4194304 | tf_op jit(solution)/shard_map/all_to_all | solution.py:496
  32.4 45.5 %copy-start = (f32[5,512]{1,0:T(8,128)S(1)}, f32[5,512]{1,0:T(8,128)}, u32[]{:S(2)}) copy-start(f32[5,512]{1,0:T(8,128)} %refs_5_.7) | copy-start | bytes 30724
  32.4 45.5 %copy-start.1 = (s32[2048]{0:T(1024)S(1)}, s32[2048]{0:T(1024)}, u32[]{:S(2)}) copy-start(s32[2048]{0:T(1024)} %refs_11_.3) | copy-start | bytes 24580
  32.4 45.5 %copy-start.2 = (s32[2048]{0:T(1024)S(1)}, s32[2048]{0:T(1024)}, u32[]{:S(2)}) copy-start(s32[2048]{0:T(1024)} %refs_10_.3) | copy-start | bytes 24580
  89.6 9.3 %collective-permute-start.2 = (bf16[512,128]{1,0:T(8,128)(2,1)S(1)}, bf16[512,128]{1,0:T(8,128)(2,1)S(1)}, u32[]{:S(2)}, u32[]{:S(2)}) collective-permute-start(bf16[512,128]{1,0:T(8,128)(2,1)S(1)} %get-tuple-element.55), channel_id=1, source_target_pairs={{0,1},{1,2},{2,3},{3,4},{4,5},{5,6},{6,7},{7,8},{8,9},{9,10},{10,1... | collective-permute-start | bytes 393224 | tf_op jit(solution)/shard_map/ppermute | solution.py:390
  89.8 9.1 %collective-permute-start.3 = (bf16[512,128]{1,0:T(8,128)(2,1)S(1)}, bf16[512,128]{1,0:T(8,128)(2,1)S(1)}, u32[]{:S(2)}, u32[]{:S(2)}) collective-permute-start(bf16[512,128]{1,0:T(8,128)(2,1)S(1)} %get-tuple-element.56), channel_id=1, source_target_pairs={{1,0},{2,1},{3,2},{4,3},{5,4},{6,5},{7,6},{8,7},{9,8},{10,9},{11,1... | collective-permute-start | bytes 393224 | tf_op jit(solution)/shard_map/ppermute | solution.py:391

commit v4 on v3

--- a/solution.py
+++ b/solution.py
@@ -34,7 +34,10 @@
 
 
 def swish(values):
-    half = values * 0.5
+    return swish_of_half(values * 0.5)
+
+
+def swish_of_half(half):
     return half * jnp.tanh(half) + half
 
 
@@ -45,14 +48,14 @@
     return (values - mean) * lax.rsqrt(var + eps) * gain
 
 
-def pick_rows(index_row, count):
+def pick_rows(index_row, count, value=1):
     rows = lax.broadcasted_iota(jnp.int16, (count, index_row.shape[1]), 0)
-    return jnp.where(rows == index_row.astype(jnp.int16), bf16(1), bf16(0))
-
-
-def pick_columns(index_column, count):
+    return jnp.where(rows == index_row.astype(jnp.int16), bf16(value), bf16(0))
+
+
+def pick_columns(index_column, count, value=1):
     columns = lax.broadcasted_iota(jnp.int16, (index_column.shape[0], count), 1)
-    return jnp.where(columns == index_column.astype(jnp.int16), bf16(1), bf16(0))
+    return jnp.where(columns == index_column.astype(jnp.int16), bf16(value), bf16(0))
 
 
 def blocks(total):
@@ -94,6 +97,16 @@
 def index_column(index, part):
     row = index_row(index, part).astype(f32)
     return jnp.transpose(jnp.broadcast_to(row, (8, row.shape[1])))[:, :1].astype(jnp.int32)
+
+
+def stagger(parts, first, second):
+    waiting = None
+    for part in parts:
+        values = first(part)
+        if waiting is not None:
+            second(*waiting)
+        waiting = (part, values)
+    second(*waiting)
 
 
 def place():
@@ -126,11 +139,12 @@
         values = norm_columns(nn(second_w()[...], hidden), column(gains(), 0)).astype(bf16)
         latent[:, part] = values
         table[:, part] = nn(send_w()[...], values).astype(bf16)
-    bias = column(biases(), 1)
+    bias = column(biases(), 1) * 0.5
+    half_w = geom_w()[...] * bf16(0.5)
     for part in blocks(geom().shape[1]):
         own = index_row(send_index(), part) - place() * cells
-        terms = nn(table[...], pick_rows(own, cells))
-        own_terms[:, part] = terms + tn(geom_w()[...], geom()[:, part]) + bias
+        terms = nn(table[...], pick_rows(own, cells, 0.5))
+        own_terms[:, part] = terms + tn(half_w, geom()[:, part]) + bias
         sums[:, part] = pick_rows(index_row(recv_index(), part) - place() * nodes, nodes)
     row_columns = jnp.transpose(rows()[...].astype(f32)).astype(jnp.int32)
     per_row, count = row_columns.shape
@@ -171,11 +185,16 @@
     )
     halo = nn(send_w[...], halo).astype(bf16)
     gain = column(gains, 1)
-    for part in blocks(own_terms.shape[1]):
+
+    def first(part):
         index = outside(index_row(send_index, part) - place() * cells, cells, reach)
-        pre_act = own_terms[:, part] + nn(halo, pick_rows(index, 2 * reach))
-        hidden = swish(pre_act).astype(bf16)
-        messages[:, part] = norm_columns(nn(edge_w[...], hidden), gain).astype(bf16)
+        half = own_terms[:, part] + nn(halo, pick_rows(index, 2 * reach, 0.5))
+        return nn(edge_w[...], swish_of_half(half).astype(bf16))
+
+    def second(part, values):
+        messages[:, part] = norm_columns(values, gain).astype(bf16)
+
+    stagger(blocks(own_terms.shape[1]), first, second)
     nodes = nt(sums[...], messages[...]).astype(bf16)
     nodes_near[...] = nodes
     copies.append(pltpu.make_async_copy(nodes_near, latent, semaphores.at[1]))
@@ -219,7 +238,7 @@
         picked = pick_columns(picked, nodes.shape[0])
         picked = nn(picked, nodes).astype(bf16)
         terms = nt(picked, recv_w()[...]) + tn(mesh_geom()[:, part], mesh_geom_w()[...])
-        recv_terms[part, :] = terms + recv_bias
+        recv_terms[part, :] = (terms + recv_bias) * 0.5
     node_terms[...] = nt(node_w()[...], nodes) + column(biases(), 3)
     latent_columns[...] = jnp.transpose(nodes.astype(f32)).astype(bf16)
     cell_bias = column(biases(), 4)
@@ -229,7 +248,8 @@
         out_terms[:, part] = nn(out_w()[...], cells) + out_bias
         terms = nn(decode_w()[...], cells) + cell_bias
         for k in range(cell_terms.shape[0]):
-            cell_terms[k, :, part] = terms + tn(cell_geom_w()[...], cell_geom()[k, :, part])
+            whole = terms + tn(cell_geom_w()[...], cell_geom()[k, :, part])
+            cell_terms[k, :, part] = whole * 0.5
 
 
 def mesh_kernel(edge_w, *refs):
@@ -245,11 +265,12 @@
     sums = []
     for i in range(len(parts) + ahead):
         if i < len(parts):
-            picks = pick_columns(index_column(slot_index, parts[i]), arrived.shape[0])
+            picks = pick_columns(index_column(slot_index, parts[i]), arrived.shape[0], 0.5)
             gathered[parts[i], :] = nn(picks, arrived[...])
         if i >= ahead:
             part = parts[i - ahead]
-            hidden = swish(gathered[part, :] + recv_terms[i - ahead]()[...]).astype(bf16)
+            half = gathered[part, :] + recv_terms[i - ahead]()[...]
+            hidden = swish_of_half(half).astype(bf16)
             messages[:, part] = norm_columns(nt(edge_w()[...], hidden), gain).astype(bf16)
             index = index_row(recv_index, part) - place() * count
             sums.append(pick_rows(index, count))
@@ -272,7 +293,7 @@
     for k in range(out.shape[0]):
         for part in blocks(out.shape[2]):
             picks = index()[k, :, part] - place() * send.shape[1]
-            picks = pick_rows(picks, send.shape[1])
+            picks = pick_rows(picks, send.shape[1], 0.5)
             out[k, :, part] = terms[k]()[:, part] + nn(send[...], picks)
 
 
@@ -296,16 +317,24 @@
     offset = out_bias[...].reshape(1, -1)
     offset = jnp.transpose(jnp.broadcast_to(offset, (8, offset.shape[1])))[:, :1]
     copies = []
-    for part in blocks(terms.shape[2]):
-        total = None
-        for k in range(terms.shape[0]):
-            count = 2 * halo.shape[1]
-            picks = outside(index[k, :, part] - place() * count, count, halo.shape[1] // 2)
-            picks = pick_rows(picks, halo.shape[1])
-            hidden = swish(terms[k, :, part] + nn(halo, picks)).astype(bf16)
-            message = norm_columns(nn(edge_w[...], hidden), gain).astype(bf16).astype(f32)
-            total = message if total is None else total + message
-        pre_act = out_terms[:, part] + nn(gathered_w[...], total.astype(bf16))
+    totals = {}
+    last = terms.shape[0] - 1
+
+    def first(spot):
+        part, k = spot
+        count = 2 * halo.shape[1]
+        picks = outside(index[k, :, part] - place() * count, count, halo.shape[1] // 2)
+        half = terms[k, :, part] + nn(halo, pick_rows(picks, halo.shape[1], 0.5))
+        return nn(edge_w[...], swish_of_half(half).astype(bf16))
+
+    def second(spot, values):
+        part, k = spot
+        message = norm_columns(values, gain).astype(bf16).astype(f32)
+        totals[part.start] = message if k == 0 else totals[part.start] + message
+        if k < last:
+            return
+        total = totals[part.start].astype(bf16)
+        pre_act = out_terms[:, part] + nn(gathered_w[...], total)
         hidden = swish(pre_act).astype(bf16)
         staged[:, part] = nn(out_w[...], hidden) + offset
         copies.append(
@@ -314,6 +343,9 @@
             )
         )
         copies[-1].start()
+
+    spots = [(part, k) for part in blocks(terms.shape[2]) for k in range(last + 1)]
+    stagger(spots, first, second)
     for copy in copies:
         copy.wait()
 

time: 107 us -> 105 us (0.981)
  Pallas kernels: 48.2 us -> 47 us
    pallas_call x6, Pallas kernels: 48.2 us -> 47 us  [fetching(): pl.pallas_call(run, out_shape=tuple(outs) + tuple((pltpu.VMEM(*shapes[i])...]
where the time goes in v4:
time: 105 us
  Pallas kernels  47 us (45%)
  waiting for transfers between devices  36.1 us (34%)
  starting transfers between devices  15.7 us (15%)
  local copies, waits for them, and re-layouts  5.33 us (5%)
    pallas_call x6, Pallas kernels, fetching(): pl.pallas_call(run, out_shape=tuple(outs) + tuple((pltpu.VMEM(*shapes[i])...  47 us
    all_to_all x1, waiting for transfers between devices, body(): lax.all_to_all(outgoing.reshape(mesh_rows.shape + (width,)), ('space', 'c...  34 us
    ppermute x2, starting transfers between devices, exchange(): high = lax.ppermute(low_end, axes, down)  11.6 us
    all_to_all x1, starting transfers between devices, body(): lax.all_to_all(outgoing.reshape(mesh_rows.shape + (width,)), ('space', 'c...  3.85 us
    reshape x2, local copies, waits for them, and re-layouts, body(): cell_geom = m2g_geom.reshape(-1, cells, per_cell).transpose(2, 0, 1)  3.18 us
  transfers between devices with their start and end apart: 5, of which 2 were waited for; matrix products, arithmetic and copies ran while one was open for 4% of the time, Pallas kernels for 21%

profile of v4, /device:TPU:0, one launch (start us, length us, event | category | flops | bytes accessed | tf_op | source)
XLA Modules:
  0.0 105.1 jit_solution(12675035861640073634)
XLA Ops:
  0.6 1.0 fusion
  1.6 6.5 %collective-permute-start.1 = (bf16[227,256]{1,0:T(8,128)(2,1)S(1)}, bf16[227,256]{1,0:T(8,128)(2,1)S(1)}, u32[]{:S(2)}, u32[]{:S(2)}) collective-permute-start(bf16[227,256]{1,0:T(8,128)(2,1)S(1)} %get-tuple-element.70), channel_id=1, source_target_pairs={{1,0},{2,1},{3,2},{4,3},{5,4},{6,5},{7,6},{8,7},{9,8},{10,9},{11,1... | collective-permute-start | bytes 348680 | tf_op jit(solution)/shard_map/ppermute | solution.py:423
  8.1 0.0 collective-permute-start
  8.1 7.0 %shard_map.194 = (bf16[512,1024]{1,0:T(8,128)(2,1)S(1)}, f32[512,1536]{1,0:T(8,128)S(1)}, bf16[512,1536]{1,0:T(8,128)(2,1)S(1)}, bf16[2048,512]{1,0:T(8,128)(2,1...) custom-call(bf16[227,1024]{1,0:T(8,128)(2,1)} %refs_0_.2, ...), custom_call_target="tpu_custom_call" | custom-call | tf_op jit(solution)/shard_map/pallas_call | solution.py:401
  15.1 0.0 collective-permute-done.1.refs_5_
  15.1 2.0 %collective-permute-done.refs_4_ = bf16[227,256]{1,0:T(8,128)(2,1)S(1)} collective-permute-done((bf16[227,256]{1,0:T(8,128)(2,1)S(1)}, bf16[227,256]{1,0:T(8,128)(2,1)S(1)}, u32[]{:S(2)}, u32[]{:S(2)}) %collective-permute-start) | collective-permute-done | bytes 116256 | tf_op jit(solution)/shard_map/ppermute | solution.py:422
  17.2 6.6 %shard_map.195 = (bf16[512,1024]{1,0:T(8,128)(2,1)}, bf16[512,512]{1,0:T(8,128)(2,1)}, bf16[2048,512]{1,0:T(8,128)(2,1)}) custom-call(bf16[512,1024]{1,0:T(8,128)(2,1)S(1)} %get-tuple-element.36.refs_0_, f32[512,1536]{1,0:T(8,128)S(1)} %get-tuple-element.37.refs_1_, bf16[512,1536]{1,0:T(8,128)(2,1)S(1)} %get-tuple-element.38.refs_2_, ...), custom_call_target="tpu_custom_call" | custom-call | tf_op jit(solution)/shard_map/pallas_call | solution.py:401
  23.8 0.0 copy-start.4
  23.8 0.0 copy-start.3
  23.8 3.9 %all-to-all-start = ((bf16[32,64,512]{2,1,0:T(8,128)(2,1)}), bf16[32,64,512]{2,1,0:T(8,128)(2,1)S(1)}, u32[]{:S(2)}, u32[]{:S(2)}) async-start(bf16[32,64,512]{2,1,0:T(8,128)(2,1)} %bitcast.7), calls=%async_computation | async-start | bytes 4194304 | tf_op jit(solution)/shard_map/all_to_all | solution.py:528
  27.7 0.3 reshape.16
  28.0 0.2 copy.21
  28.2 0.6 broadcast_in_dim.3.refs_0_
  28.8 2.2 %reshape.17 = bf16[4,1024,3]{2,1,0:T(8,128)(2,1)S(1)} reshape(bf16[4,3072]{1,0:T(4,128)(2,1)S(1)} %copy-done.3) | data formatting | bytes 49152 | tf_op jit(solution)/shard_map/reshape | solution.py:539
  31.0 1.0 copy.22
  32.0 11.5 %shard_map.196 = (f32[2048,512]{1,0:T(8,128)}, f32[512,512]{1,0:T(8,128)}, bf16[512,512]{1,0:T(8,128)(2,1)}, f32[3,512,1024]{2,1,0:T(8,128)}, f32[512,1024]{1,0:T(8,128)}) custom-call(bf16[512,512]{1,0:T(8,128)(2,1)} %get-tuple-element.49.refs_0_, bf16[4,2048]{1,0:T(4,128)(2,1)} %refs_1_.1, bf16[4,2,512,512]{3,2,1,0:T(8,128)(2,1)} %refs_6_.5, ...), custom_call_target="tpu_custom_call" | custom-call | tf_op jit(solution)/shard_map/pallas_call | solution.py:401
  43.5 34.0 %all-to-all-done = bf16[32,64,512]{2,1,0:T(8,128)(2,1)S(1)} async-done(((bf16[32,64,512]{2,1,0:T(8,128)(2,1)}), bf16[32,64,512]{2,1,0:T(8,128)(2,1)S(1)}, u32[]{:S(2)}, u32[]{:S(2)}) %all-to-all-start) | async-done | bytes 2097184 | tf_op jit(solution)/shard_map/all_to_all | solution.py:528
  77.5 11.5 %shard_map.197 = (bf16[512,512]{1,0:T(8,128)(2,1)}, bf16[512,512]{1,0:T(8,128)(2,1)S(1)}, bf16[512,128]{1,0:T(8,128)(2,1)S(1)}, bf16[512,128]{1,0:T(8,128)(2,1)S(1)}) custom-call(bf16[5,512,512]{2,1,0:T(8,128)(2,1)} %refs_4_.3, f32[2048,512]{1,0:T(8,128)} %get-tuple-element.51.refs_1_.refs_2_.refs_3_.refs_4_, ...), custom_call_target="tpu_custom_call" | custom-call | tf_op jit(solution)/shard_map/pallas_call | solution.py:401
  89.0 0.2 collective-permute-start.2
  89.2 5.2 %collective-permute-start.3 = (bf16[512,128]{1,0:T(8,128)(2,1)S(1)}, bf16[512,128]{1,0:T(8,128)(2,1)S(1)}, u32[]{:S(2)}, u32[]{:S(2)}) collective-permute-start(bf16[512,128]{1,0:T(8,128)(2,1)S(1)} %get-tuple-element.56), channel_id=1, source_target_pairs={{1,0},{2,1},{3,2},{4,3},{5,4},{6,5},{7,6},{8,7},{9,8},{10,9},{11,1... | collective-permute-start | bytes 393224 | tf_op jit(solution)/shard_map/ppermute | solution.py:423
  94.4 3.9 %shard_map.198 = (f32[3,512,1024]{2,1,0:T(8,128)S(1)}, s32[3,1,1024]{2,1,0:T(1,128)S(1)}, bf16[512,512]{1,0:T(8,128)(2,1)S(1)}, f32[5,512]{1,0:T(8,128)S(1)}, bf...) custom-call(s32[3,1,1024]{2,1,0:T(1,128)} %broadcast_in_dim.3.refs_0_, ...), custom_call_target="tpu_custom_call" | custom-call | tf_op jit(solution)/shard_map/pallas_call | solution.py:401
  98.3 0.0 collective-permute-done.2.refs_0_
  98.3 0.0 collective-permute-done.3.refs_1_
  98.3 6.6 %shard_map.199 = f32[227,1024]{1,0:T(8,128)} custom-call(bf16[512,128]{1,0:T(8,128)(2,1)S(1)} %collective-permute-done.2.refs_0_, bf16[512,128]{1,0:T(8,128)(2,1)S(1)} %collective-permute-done.3.refs_1_, s32[3,1,1024]{2,1,0:T(1,128)S(1)} %get-tuple-element.61.refs_2_, f32[3,512,1024]{2,1,0:T(8,128)S(1)} %get-tuple-element.62.refs_3_, ...), custom_call_target="tpu_custom_call" | custom-call | tf_op jit(solution)/shard_map/pallas_call | solution.py:401
  (8 shorter events, 0.0 us)
Async XLA Ops:
  1.6 13.5 %collective-permute-start.1 = (bf16[227,256]{1,0:T(8,128)(2,1)S(1)}, bf16[227,256]{1,0:T(8,128)(2,1)S(1)}, u32[]{:S(2)}, u32[]{:S(2)}) collective-permute-start(bf16[227,256]{1,0:T(8,128)(2,1)S(1)} %get-tuple-element.70), channel_id=1, source_target_pairs={{1,0},{2,1},{3,2},{4,3},{5,4},{6,5},{7,6},{8,7},{9,8},{10,9},{11,1... | collective-permute-start | bytes 348680 | tf_op jit(solution)/shard_map/ppermute | solution.py:423
  8.1 9.1 %collective-permute-start = (bf16[227,256]{1,0:T(8,128)(2,1)S(1)}, bf16[227,256]{1,0:T(8,128)(2,1)S(1)}, u32[]{:S(2)}, u32[]{:S(2)}) collective-permute-start(bf16[227,256]{1,0:T(8,128)(2,1)S(1)} %get-tuple-element.71), channel_id=1, source_target_pairs={{0,1},{1,2},{2,3},{3,4},{4,5},{5,6},{6,7},{7,8},{8,9},{9,10},{10,1... | collective-permute-start | bytes 348680 | tf_op jit(solution)/shard_map/ppermute | solution.py:422
  23.8 3.9 %copy-start.4 = (s32[3072]{0:T(1024)S(1)}, s32[3072]{0:T(1024)}, u32[]{:S(2)}) copy-start(s32[3072]{0:T(1024)} %param.37) | copy-start | bytes 36868
  23.8 5.0 %copy-start.3 = (bf16[4,3072]{1,0:T(4,128)(2,1)S(1)}, bf16[4,3072]{1,0:T(4,128)(2,1)}, u32[]{:S(2)}) copy-start(bf16[4,3072]{1,0:T(4,128)(2,1)} %param.31) | copy-start | bytes 73732
  23.8 53.7 %all-to-all-start = ((bf16[32,64,512]{2,1,0:T(8,128)(2,1)}), bf16[32,64,512]{2,1,0:T(8,128)(2,1)S(1)}, u32[]{:S(2)}, u32[]{:S(2)}) async-start(bf16[32,64,512]{2,1,0:T(8,128)(2,1)} %bitcast.7), calls=%async_computation | async-start | bytes 4194304 | tf_op jit(solution)/shard_map/all_to_all | solution.py:528
  32.0 45.5 %copy-start = (f32[5,512]{1,0:T(8,128)S(1)}, f32[5,512]{1,0:T(8,128)}, u32[]{:S(2)}) copy-start(f32[5,512]{1,0:T(8,128)} %refs_5_.7) | copy-start | bytes 30724
  32.0 45.5 %copy-start.1 = (s32[2048]{0:T(1024)S(1)}, s32[2048]{0:T(1024)}, u32[]{:S(2)}) copy-start(s32[2048]{0:T(1024)} %refs_11_.3) | copy-start | bytes 24580
  32.0 45.5 %copy-start.2 = (s32[2048]{0:T(1024)S(1)}, s32[2048]{0:T(1024)}, u32[]{:S(2)}) copy-start(s32[2048]{0:T(1024)} %refs_10_.3) | copy-start | bytes 24580
  89.0 9.3 %collective-permute-start.2 = (bf16[512,128]{1,0:T(8,128)(2,1)S(1)}, bf16[512,128]{1,0:T(8,128)(2,1)S(1)}, u32[]{:S(2)}, u32[]{:S(2)}) collective-permute-start(bf16[512,128]{1,0:T(8,128)(2,1)S(1)} %get-tuple-element.55), channel_id=1, source_target_pairs={{0,1},{1,2},{2,3},{3,4},{4,5},{5,6},{6,7},{7,8},{8,9},{9,10},{10,1... | collective-permute-start | bytes 393224 | tf_op jit(solution)/shard_map/ppermute | solution.py:422
  89.2 9.1 %collective-permute-start.3 = (bf16[512,128]{1,0:T(8,128)(2,1)S(1)}, bf16[512,128]{1,0:T(8,128)(2,1)S(1)}, u32[]{:S(2)}, u32[]{:S(2)}) collective-permute-start(bf16[512,128]{1,0:T(8,128)(2,1)S(1)} %get-tuple-element.56), channel_id=1, source_target_pairs={{1,0},{2,1},{3,2},{4,3},{5,4},{6,5},{7,6},{8,7},{9,8},{10,9},{11,1... | collective-permute-start | bytes 393224 | tf_op jit(solution)/shard_map/ppermute | solution.py:423

commit v5 on v4

--- a/solution.py
+++ b/solution.py
@@ -134,17 +134,23 @@
     bias = column(biases(), 0)
     cells = x().shape[1]
     nodes = sums.shape[0]
-    for part in blocks(cells):
+
+    def first(part):
         hidden = swish(tn(embed_w()[...], x()[:, part]) + bias).astype(bf16)
-        values = norm_columns(nn(second_w()[...], hidden), column(gains(), 0)).astype(bf16)
+        return nn(second_w()[...], hidden)
+
+    def second(part, values):
+        values = norm_columns(values, column(gains(), 0)).astype(bf16)
         latent[:, part] = values
         table[:, part] = nn(send_w()[...], values).astype(bf16)
-    bias = column(biases(), 1) * 0.5
+
+    stagger(blocks(cells), first, second)
+    edge_bias = column(biases(), 1) * 0.5
     half_w = geom_w()[...] * bf16(0.5)
     for part in blocks(geom().shape[1]):
         own = index_row(send_index(), part) - place() * cells
         terms = nn(table[...], pick_rows(own, cells, 0.5))
-        own_terms[:, part] = terms + tn(half_w, geom()[:, part]) + bias
+        own_terms[:, part] = terms + tn(half_w, geom()[:, part]) + edge_bias
         sums[:, part] = pick_rows(index_row(recv_index(), part) - place() * nodes, nodes)
     row_columns = jnp.transpose(rows()[...].astype(f32)).astype(jnp.int32)
     per_row, count = row_columns.shape
@@ -262,6 +268,7 @@
     parts = blocks(messages.shape[1])
     gain = column(gains, 2)
     ahead = 2
+    waiting = None
     sums = []
     for i in range(len(parts) + ahead):
         if i < len(parts):
@@ -271,9 +278,13 @@
             part = parts[i - ahead]
             half = gathered[part, :] + recv_terms[i - ahead]()[...]
             hidden = swish_of_half(half).astype(bf16)
-            messages[:, part] = norm_columns(nt(edge_w()[...], hidden), gain).astype(bf16)
+            values = nt(edge_w()[...], hidden)
             index = index_row(recv_index, part) - place() * count
             sums.append(pick_rows(index, count))
+            if waiting is not None:
+                messages[:, waiting[0]] = norm_columns(waiting[1], gain).astype(bf16)
+            waiting = (part, values)
+    messages[:, waiting[0]] = norm_columns(waiting[1], gain).astype(bf16)
     nodes = nt(jnp.concatenate(sums, axis=1), messages[...]).astype(bf16)
     hidden = swish(nt(node_w()[...], nodes) + node_terms()[...]).astype(bf16)
     normed = norm_columns(nn(node_second_w()[...], hidden), column(gains, 3))

time: 105 us -> 105 us (level)
  no operation moved by 1% of the time
where the time goes in v5:
time: 105 us
  Pallas kernels  46.6 us (44%)
  waiting for transfers between devices  36.4 us (35%)
  starting transfers between devices  15.4 us (15%)
  local copies, waits for them, and re-layouts  5.33 us (5%)
    pallas_call x6, Pallas kernels, fetching(): pl.pallas_call(run, out_shape=tuple(outs) + tuple((pltpu.VMEM(*shapes[i])...  46.6 us
    all_to_all x1, waiting for transfers between devices, body(): lax.all_to_all(outgoing.reshape(mesh_rows.shape + (width,)), ('space', 'c...  34 us
    ppermute x2, starting transfers between devices, exchange(): high = lax.ppermute(low_end, axes, down)  11.7 us
    all_to_all x1, starting transfers between devices, body(): lax.all_to_all(outgoing.reshape(mesh_rows.shape + (width,)), ('space', 'c...  3.55 us
    reshape x2, local copies, waits for them, and re-layouts, body(): cell_geom = m2g_geom.reshape(-1, cells, per_cell).transpose(2, 0, 1)  3.18 us
    ppermute x2, waiting for transfers between devices, exchange(): low = lax.ppermute(high_end, axes, up)  2.36 us
  transfers between devices with their start and end apart: 5, of which 2 were waited for; matrix products, arithmetic and copies ran while one was open for 4% of the time, Pallas kernels for 21%

profile of v5, /device:TPU:0, one launch (start us, length us, event | category | flops | bytes accessed | tf_op | source)
XLA Modules:
  0.0 104.7 jit_solution(11914495909360072166)
XLA Ops:
  0.6 1.0 fusion
  1.6 6.5 %collective-permute-start.1 = (bf16[227,256]{1,0:T(8,128)(2,1)S(1)}, bf16[227,256]{1,0:T(8,128)(2,1)S(1)}, u32[]{:S(2)}, u32[]{:S(2)}) collective-permute-start(bf16[227,256]{1,0:T(8,128)(2,1)S(1)} %get-tuple-element.70), channel_id=1, source_target_pairs={{1,0},{2,1},{3,2},{4,3},{5,4},{6,5},{7,6},{8,7},{9,8},{10,9},{11,1... | collective-permute-start | bytes 348680 | tf_op jit(solution)/shard_map/ppermute | solution.py:434
  8.1 0.0 collective-permute-start
  8.1 6.7 %shard_map.194 = (bf16[512,1024]{1,0:T(8,128)(2,1)S(1)}, f32[512,1536]{1,0:T(8,128)S(1)}, bf16[512,1536]{1,0:T(8,128)(2,1)S(1)}, bf16[2048,512]{1,0:T(8,128)(2,1...) custom-call(bf16[227,1024]{1,0:T(8,128)(2,1)} %refs_0_.2, ...), custom_call_target="tpu_custom_call" | custom-call | tf_op jit(solution)/shard_map/pallas_call | solution.py:412
  14.8 0.0 collective-permute-done.1.refs_5_
  14.8 2.4 %collective-permute-done.refs_4_ = bf16[227,256]{1,0:T(8,128)(2,1)S(1)} collective-permute-done((bf16[227,256]{1,0:T(8,128)(2,1)S(1)}, bf16[227,256]{1,0:T(8,128)(2,1)S(1)}, u32[]{:S(2)}, u32[]{:S(2)}) %collective-permute-start) | collective-permute-done | bytes 116256 | tf_op jit(solution)/shard_map/ppermute | solution.py:433
  17.2 6.6 %shard_map.195 = (bf16[512,1024]{1,0:T(8,128)(2,1)}, bf16[512,512]{1,0:T(8,128)(2,1)}, bf16[2048,512]{1,0:T(8,128)(2,1)}) custom-call(bf16[512,1024]{1,0:T(8,128)(2,1)S(1)} %get-tuple-element.36.refs_0_, f32[512,1536]{1,0:T(8,128)S(1)} %get-tuple-element.37.refs_1_, bf16[512,1536]{1,0:T(8,128)(2,1)S(1)} %get-tuple-element.38.refs_2_, ...), custom_call_target="tpu_custom_call" | custom-call | tf_op jit(solution)/shard_map/pallas_call | solution.py:412
  23.8 0.0 copy-start.4
  23.8 0.0 copy-start.3
  23.8 3.5 %all-to-all-start = ((bf16[32,64,512]{2,1,0:T(8,128)(2,1)}), bf16[32,64,512]{2,1,0:T(8,128)(2,1)S(1)}, u32[]{:S(2)}, u32[]{:S(2)}) async-start(bf16[32,64,512]{2,1,0:T(8,128)(2,1)} %bitcast.7), calls=%async_computation | async-start | bytes 4194304 | tf_op jit(solution)/shard_map/all_to_all | solution.py:539
  27.4 0.3 reshape.16
  27.7 0.2 copy.21
  27.9 0.6 broadcast_in_dim.3.refs_0_
  28.5 2.2 %reshape.17 = bf16[4,1024,3]{2,1,0:T(8,128)(2,1)S(1)} reshape(bf16[4,3072]{1,0:T(4,128)(2,1)S(1)} %copy-done.3) | data formatting | bytes 49152 | tf_op jit(solution)/shard_map/reshape | solution.py:550
  30.7 1.0 copy.22
  31.7 11.5 %shard_map.196 = (f32[2048,512]{1,0:T(8,128)}, f32[512,512]{1,0:T(8,128)}, bf16[512,512]{1,0:T(8,128)(2,1)}, f32[3,512,1024]{2,1,0:T(8,128)}, f32[512,1024]{1,0:T(8,128)}) custom-call(bf16[512,512]{1,0:T(8,128)(2,1)} %get-tuple-element.49.refs_0_, bf16[4,2048]{1,0:T(4,128)(2,1)} %refs_1_.1, bf16[4,2,512,512]{3,2,1,0:T(8,128)(2,1)} %refs_6_.5, ...), custom_call_target="tpu_custom_call" | custom-call | tf_op jit(solution)/shard_map/pallas_call | solution.py:412
  43.2 34.0 %all-to-all-done = bf16[32,64,512]{2,1,0:T(8,128)(2,1)S(1)} async-done(((bf16[32,64,512]{2,1,0:T(8,128)(2,1)}), bf16[32,64,512]{2,1,0:T(8,128)(2,1)S(1)}, u32[]{:S(2)}, u32[]{:S(2)}) %all-to-all-start) | async-done | bytes 2097184 | tf_op jit(solution)/shard_map/all_to_all | solution.py:539
  77.2 11.3 %shard_map.197 = (bf16[512,512]{1,0:T(8,128)(2,1)}, bf16[512,512]{1,0:T(8,128)(2,1)S(1)}, bf16[512,128]{1,0:T(8,128)(2,1)S(1)}, bf16[512,128]{1,0:T(8,128)(2,1)S(1)}) custom-call(bf16[5,512,512]{2,1,0:T(8,128)(2,1)} %refs_4_.3, f32[2048,512]{1,0:T(8,128)} %get-tuple-element.51.refs_1_.refs_2_.refs_3_.refs_4_, ...), custom_call_target="tpu_custom_call" | custom-call | tf_op jit(solution)/shard_map/pallas_call | solution.py:412
  88.6 0.2 collective-permute-start.2
  88.8 5.2 %collective-permute-start.3 = (bf16[512,128]{1,0:T(8,128)(2,1)S(1)}, bf16[512,128]{1,0:T(8,128)(2,1)S(1)}, u32[]{:S(2)}, u32[]{:S(2)}) collective-permute-start(bf16[512,128]{1,0:T(8,128)(2,1)S(1)} %get-tuple-element.56), channel_id=1, source_target_pairs={{1,0},{2,1},{3,2},{4,3},{5,4},{6,5},{7,6},{8,7},{9,8},{10,9},{11,1... | collective-permute-start | bytes 393224 | tf_op jit(solution)/shard_map/ppermute | solution.py:434
  94.0 3.9 %shard_map.198 = (f32[3,512,1024]{2,1,0:T(8,128)S(1)}, s32[3,1,1024]{2,1,0:T(1,128)S(1)}, bf16[512,512]{1,0:T(8,128)(2,1)S(1)}, f32[5,512]{1,0:T(8,128)S(1)}, bf...) custom-call(s32[3,1,1024]{2,1,0:T(1,128)} %broadcast_in_dim.3.refs_0_, ...), custom_call_target="tpu_custom_call" | custom-call | tf_op jit(solution)/shard_map/pallas_call | solution.py:412
  97.9 0.0 collective-permute-done.2.refs_0_
  97.9 0.0 collective-permute-done.3.refs_1_
  97.9 6.6 %shard_map.199 = f32[227,1024]{1,0:T(8,128)} custom-call(bf16[512,128]{1,0:T(8,128)(2,1)S(1)} %collective-permute-done.2.refs_0_, bf16[512,128]{1,0:T(8,128)(2,1)S(1)} %collective-permute-done.3.refs_1_, s32[3,1,1024]{2,1,0:T(1,128)S(1)} %get-tuple-element.61.refs_2_, f32[3,512,1024]{2,1,0:T(8,128)S(1)} %get-tuple-element.62.refs_3_, ...), custom_call_target="tpu_custom_call" | custom-call | tf_op jit(solution)/shard_map/pallas_call | solution.py:412
  (8 shorter events, 0.0 us)
Async XLA Ops:
  1.6 13.2 %collective-permute-start.1 = (bf16[227,256]{1,0:T(8,128)(2,1)S(1)}, bf16[227,256]{1,0:T(8,128)(2,1)S(1)}, u32[]{:S(2)}, u32[]{:S(2)}) collective-permute-start(bf16[227,256]{1,0:T(8,128)(2,1)S(1)} %get-tuple-element.70), channel_id=1, source_target_pairs={{1,0},{2,1},{3,2},{4,3},{5,4},{6,5},{7,6},{8,7},{9,8},{10,9},{11,1... | collective-permute-start | bytes 348680 | tf_op jit(solution)/shard_map/ppermute | solution.py:434
  8.1 9.1 %collective-permute-start = (bf16[227,256]{1,0:T(8,128)(2,1)S(1)}, bf16[227,256]{1,0:T(8,128)(2,1)S(1)}, u32[]{:S(2)}, u32[]{:S(2)}) collective-permute-start(bf16[227,256]{1,0:T(8,128)(2,1)S(1)} %get-tuple-element.71), channel_id=1, source_target_pairs={{0,1},{1,2},{2,3},{3,4},{4,5},{5,6},{6,7},{7,8},{8,9},{9,10},{10,1... | collective-permute-start | bytes 348680 | tf_op jit(solution)/shard_map/ppermute | solution.py:433
  23.8 3.6 %copy-start.4 = (s32[3072]{0:T(1024)S(1)}, s32[3072]{0:T(1024)}, u32[]{:S(2)}) copy-start(s32[3072]{0:T(1024)} %param.37) | copy-start | bytes 36868
  23.8 4.7 %copy-start.3 = (bf16[4,3072]{1,0:T(4,128)(2,1)S(1)}, bf16[4,3072]{1,0:T(4,128)(2,1)}, u32[]{:S(2)}) copy-start(bf16[4,3072]{1,0:T(4,128)(2,1)} %param.31) | copy-start | bytes 73732
  23.8 53.4 %all-to-all-start = ((bf16[32,64,512]{2,1,0:T(8,128)(2,1)}), bf16[32,64,512]{2,1,0:T(8,128)(2,1)S(1)}, u32[]{:S(2)}, u32[]{:S(2)}) async-start(bf16[32,64,512]{2,1,0:T(8,128)(2,1)} %bitcast.7), calls=%async_computation | async-start | bytes 4194304 | tf_op jit(solution)/shard_map/all_to_all | solution.py:539
  31.7 45.5 %copy-start = (f32[5,512]{1,0:T(8,128)S(1)}, f32[5,512]{1,0:T(8,128)}, u32[]{:S(2)}) copy-start(f32[5,512]{1,0:T(8,128)} %refs_5_.7) | copy-start | bytes 30724
  31.7 45.5 %copy-start.1 = (s32[2048]{0:T(1024)S(1)}, s32[2048]{0:T(1024)}, u32[]{:S(2)}) copy-start(s32[2048]{0:T(1024)} %refs_11_.3) | copy-start | bytes 24580
  31.7 45.5 %copy-start.2 = (s32[2048]{0:T(1024)S(1)}, s32[2048]{0:T(1024)}, u32[]{:S(2)}) copy-start(s32[2048]{0:T(1024)} %refs_10_.3) | copy-start | bytes 24580
  88.6 9.3 %collective-permute-start.2 = (bf16[512,128]{1,0:T(8,128)(2,1)S(1)}, bf16[512,128]{1,0:T(8,128)(2,1)S(1)}, u32[]{:S(2)}, u32[]{:S(2)}) collective-permute-start(bf16[512,128]{1,0:T(8,128)(2,1)S(1)} %get-tuple-element.55), channel_id=1, source_target_pairs={{0,1},{1,2},{2,3},{3,4},{4,5},{5,6},{6,7},{7,8},{8,9},{9,10},{10,1... | collective-permute-start | bytes 393224 | tf_op jit(solution)/shard_map/ppermute | solution.py:433
  88.8 9.1 %collective-permute-start.3 = (bf16[512,128]{1,0:T(8,128)(2,1)S(1)}, bf16[512,128]{1,0:T(8,128)(2,1)S(1)}, u32[]{:S(2)}, u32[]{:S(2)}) collective-permute-start(bf16[512,128]{1,0:T(8,128)(2,1)S(1)} %get-tuple-element.56), channel_id=1, source_target_pairs={{1,0},{2,1},{3,2},{4,3},{5,4},{6,5},{7,6},{8,7},{9,8},{10,9},{11,1... | collective-permute-start | bytes 393224 | tf_op jit(solution)/shard_map/ppermute | solution.py:434
